TPU v7x, 256 devices: a whole 4x4x8 slice. The times are simulated.
256 devices in a mesh: seq: 128 (over y, x_hi, z, core), kv: 2 (over x_lo).
Axes of the slice: x: 4 (x_hi: 2, x_lo: 2; x = x_hi * 2 + x_lo), y: 4, z: 8, core: 2. Of those that a mesh axis runs over, the one named last changes fastest.
Arguments:
- queries: bfloat16 [32768, 32, 128], P('seq', 'kv'), may hold values from -6 to 6
- keys: bfloat16 [32768, 16, 128], P('seq', 'kv'), may hold values from -6 to 6
- values: bfloat16 [32768, 16, 128], P('seq', 'kv'), may hold values from -6 to 6
- output_gradient: bfloat16 [32768, 32, 128], P('seq', 'kv'), may hold values from -288 to 288
- window_start: int32 [32768], P('seq'), may hold values from 0 to 32767, as said below
- query_gain: float32 [128], replicated, may hold values from 0.1 to 1.9
- key_gain: float32 [128], replicated, may hold values from 0.1 to 1.9
Outputs:
- query_grad: bfloat16 [32768, 32, 128], P('seq', 'kv')
- key_grad: bfloat16 [32768, 16, 128], P('seq', 'kv')
- value_grad: bfloat16 [32768, 16, 128], P('seq', 'kv')
- query_gain_grad: float32 [128], replicated
- key_gain_grad: float32 [128], replicated
Inputs may be any that keep to these rules, and one draw needn't show every extreme that they name: window_start[t] = max(first position of token t's document, t - 1023); documents are runs of consecutive tokens, the last token begins a document of its own, and t - window_start[t] equals 1023 for some token.
All inputs are finite; a program needn't handle non-finite values.
Results may differ from a plain program's by a relative error of at most 0.014.
Values may be sent and summed in bfloat16 or wider, within the bound.
No kernel may reach another device: no remote copies, remote signals or barrier semaphores. Data moves between devices by JAX's collectives and lax.ppermute only.
A program may use at most 128 MiB of HBM per device.

v0:
```python
import functools
import math

import jax
import jax.numpy as jnp
from jax import lax
from jax.experimental import pallas as pl
from jax.experimental.pallas import tpu as pltpu
from jax.sharding import PartitionSpec as P


WINDOW_LENGTH = 1024
CHUNKS = 2
attn_scale = 168.0 ** (-0.5)
norm_eps = 1e-06
rope_base = 10000.0
query_scale = attn_scale * math.log2(math.e)
VMEM_LIMIT = 60 * 1024 * 1024
HALF = 128
bf16 = jnp.bfloat16
f32 = jnp.float32


def hop(value, steps):
    count = lax.axis_size("seq")
    first, last = max(0, -steps), min(count, count - steps)
    return lax.ppermute(value, "seq", [(s, s + steps) for s in range(first, last)])


def swap(value):
    return lax.ppermute(value, "seq", [(s, s ^ 1) for s in range(lax.axis_size("seq"))])


def all_sum(value):
    count = lax.axis_size("seq") * lax.axis_size("kv")
    bits = [1 << i for i in range(count.bit_length() - 1)]
    order = [2, 4, 8, 16, 1, 32, 64, 128] if count == 256 else bits
    for i in range(0, len(order), 2):
        pair = order[i : i + 2]
        masks = pair + ([pair[0] ^ pair[1]] if len(pair) == 2 else [])
        parts = [
            lax.ppermute(value, ("seq", "kv"), [(s, s ^ m) for s in range(count)]) for m in masks
        ]
        value = functools.reduce(lambda a, b: a + b, parts, value)
    return value


def rope_tables(positions, width):
    half = width // 2
    frequency = rope_base ** (-(jnp.arange(half, dtype=f32) * 2.0) / width)
    angles = positions.astype(f32)[:, None] * frequency[None, :]
    cos, sin = jnp.cos(angles), jnp.sin(angles)
    return jnp.concatenate([cos, cos], -1), jnp.concatenate([-sin, sin], -1)


def turn(x, cos, sin):
    return x * cos + pltpu.roll(x, 64, 1) * sin


def unturn(x, cos, sin):
    return x * cos - pltpu.roll(x, 64, 1) * sin


def key_prep_kernel(k_ref, v_ref, gain_ref, cos_ref, sin_ref, *rest):
    out_refs, scr = rest[:-1], rest[-1]
    tokens, heads, width = k_ref.shape
    per = heads // len(out_refs)
    scr[0] = k_ref[...].astype(f32).reshape(tokens * heads, width)
    scr[1] = v_ref[...].astype(f32).reshape(tokens * heads, width)
    for head in range(heads):
        out = out_refs[head // per]
        x = scr[0, pl.ds(head, tokens, stride=heads), :]
        inv = lax.rsqrt(jnp.mean(x * x, axis=-1, keepdims=True) + norm_eps)
        x = x * inv * gain_ref[...]
        out[0, head % per] = turn(x, cos_ref[...], sin_ref[...]).astype(bf16)
        out[1, head % per] = scr[1, pl.ds(head, tokens, stride=heads), :].astype(bf16)


def query_prep_kernel(q_ref, g_ref, start_ref, gain_ref, cos_ref, sin_ref, qs_ref, go_ref, bias_ref, scr):
    tokens, heads, width = q_ref.shape
    scr[0] = q_ref[...].astype(f32).reshape(tokens * heads, width)
    scr[1] = g_ref[...].astype(f32).reshape(tokens * heads, width)

    def one(group, carry):
        for r in range(2):
            x = scr[0, pl.ds(2 * group + r, tokens, stride=heads), :]
            inv = lax.rsqrt(jnp.mean(x * x, axis=-1, keepdims=True) + norm_eps)
            x = x * inv * gain_ref[...]
            x = (turn(x, cos_ref[...], sin_ref[...]) * query_scale).astype(bf16)
            g = scr[1, pl.ds(2 * group + r, tokens, stride=heads), :].astype(bf16)
            for h in range(tokens // HALF):
                qs_ref[group, h, r * HALF : (r + 1) * HALF, :] = x[h * HALF : (h + 1) * HALF]
                go_ref[group, h, r * HALF : (r + 1) * HALF, :] = g[h * HALF : (h + 1) * HALF]
        return carry

    lax.fori_loop(0, heads // 2, one, 0)
    span = bias_ref.shape[1]
    for h in range(tokens // HALF):
        key = lax.broadcasted_iota(jnp.int32, (span, HALF), 0) + h * HALF
        token = lax.broadcasted_iota(jnp.int32, (span, HALF), 1) + h * HALF
        seen = (key >= start_ref[h : h + 1, :]) & (key <= token + WINDOW_LENGTH)
        bias_ref[h] = jnp.where(seen, 0.0, -1e30).astype(f32)


NT = (((1,), (1,)), ((), ()))


def dot(a, b, dims=(((1,), (0,)), ((), ()))):
    return lax.dot_general(a, b, dims, preferred_element_type=f32)


def main_kernel(
    b4, b3, b2, b1, b0, q_ref, g_ref, bias_ref, cos_ref, sin_ref,
    odd_ref, even_ref, own_ref, dq_ref, gain_ref,
    k_scr, v_scr, kt_scr, e_scr, p_scr, dk_scr, dv_scr,
):
    tokens = b0.shape[2]
    blocks = (b4, b3, b2, b1, b0)
    for i, block in enumerate(blocks):
        k_scr[i * tokens : (i + 1) * tokens, :] = block[0, 0]
        v_scr[i * tokens : (i + 1) * tokens, :] = block[1, 0]
    kt_scr[...] = k_scr[...].astype(f32).T.astype(bf16)
    dk_scr[...] = jnp.zeros_like(dk_scr)
    dv_scr[...] = jnp.zeros_like(dv_scr)
    span = bias_ref.shape[1]
    step = 384
    steps = span // step

    @pl.when(pl.program_id(0) == 0)
    def _():
        gain_ref[...] = jnp.zeros_like(gain_ref)

    def unit(h, carry):
        base = pl.multiple_of(h * HALF, HALF)
        q = q_ref[0, h]
        g = g_ref[0, h]
        total = jnp.zeros((1, 2 * HALF), f32)
        delta = jnp.zeros((1, 2 * HALF), f32)
        for j in range(steps):
            rows = pl.ds(base + j * step, step)
            s = dot(k_scr[rows, :], q, NT)
            bias = bias_ref[h, j * step : (j + 1) * step, :]
            e = jnp.exp2(s + jnp.concatenate([bias, bias], 1))
            p = dot(v_scr[rows, :], g, NT)
            total = total + jnp.sum(e, axis=0, keepdims=True)
            delta = delta + jnp.sum(e * p, axis=0, keepdims=True)
            e_scr[j * step : (j + 1) * step, :] = e
            p_scr[j * step : (j + 1) * step, :] = p
        inv = 1.0 / total
        delta = delta * inv
        dqt = jnp.zeros((128, 2 * HALF), f32)
        for j in range(steps):
            rows = pl.ds(base + j * step, step)
            w = e_scr[j * step : (j + 1) * step, :] * inv
            ds = (w * (p_scr[j * step : (j + 1) * step, :] - delta)).astype(bf16)
            dk_scr[rows, :] += dot(ds, q)
            dv_scr[rows, :] += dot(w.astype(bf16), g)
            dqt = dqt + dot(kt_scr[:, rows], ds)
        dq = (dqt * attn_scale).T
        place = pl.ds(4 * 2 * HALF + base, HALF)
        cos = jnp.concatenate([cos_ref[place, :]] * 2, 0)
        sin = jnp.concatenate([sin_ref[place, :]] * 2, 0)
        dqn = unturn(dq, cos, sin)
        dq_ref[0, h] = dqn
        qn = unturn(q.astype(f32), cos, sin)
        gain_ref[0:1, :] += jnp.sum(dqn * qn, axis=0, keepdims=True)
        return carry

    lax.fori_loop(0, tokens // HALF, unit, 0)

    def finish(i):
        rows = slice(i * tokens, (i + 1) * tokens)
        dk = dk_scr[rows, :] * math.log(2.0)
        cos, sin = cos_ref[rows, :], sin_ref[rows, :]
        kn = unturn(k_scr[rows, :].astype(f32), cos, sin)
        gain_ref[1:2, :] += jnp.sum(unturn(dk, cos, sin) * kn, axis=0, keepdims=True)
        return dk, dv_scr[rows, :]

    for i, (ref, at) in enumerate(((even_ref, 0), (odd_ref, 0), (even_ref, 1), (odd_ref, 1))):
        dk, dv = finish(i)
        ref[at, 0, 0] = dk.astype(bf16)
        ref[at, 1, 0] = dv.astype(bf16)
    dk, dv = finish(4)
    own_ref[0, 0] = dk
    own_ref[1, 0] = dv


def norm_back(dn, x, gain):
    inv = lax.rsqrt(jnp.mean(x * x, axis=-1, keepdims=True) + norm_eps)
    unit = x * inv
    gu = dn * gain
    return inv * (gu - unit * jnp.mean(gu * unit, axis=-1, keepdims=True))


def query_end_kernel(q_ref, gain_ref, *rest):
    dq_refs, out_ref, scr, res = rest[:-3], rest[-3], rest[-2], rest[-1]
    tokens, heads, width = q_ref.shape
    scr[...] = q_ref[...].astype(f32).reshape(tokens * heads, width)
    per = dq_refs[0].shape[0]
    for c, dq_ref in enumerate(dq_refs):

        def one(i, carry, c=c, dq_ref=dq_ref):
            for r in range(2):
                rows = pl.ds(2 * (c * per + i) + r, tokens, stride=heads)
                dn = jnp.concatenate(
                    [dq_ref[i, h, r * HALF : (r + 1) * HALF, :] for h in range(tokens // HALF)], 0
                )
                res[rows, :] = norm_back(dn, scr[rows, :], gain_ref[...])
            return carry

        lax.fori_loop(0, per, one, 0)
    out_ref[...] = res[...].reshape(tokens, heads, width).astype(bf16)


def key_end_kernel(low_ref, k_ref, gain_ref, cos_ref, sin_ref, *rest):
    kg_ref, vg_ref, scr, res = rest[-4:]
    parts = rest[:-4]
    tokens, heads, width = k_ref.shape
    scr[...] = k_ref[...].astype(f32).reshape(tokens * heads, width)
    per = parts[0].shape[1]
    low = low_ref[0]
    for c in range(len(parts) // 3):
        own, other, came = parts[3 * c : 3 * c + 3]
        for i in range(per):
            rows = pl.ds(c * per + i, tokens, stride=heads)
            dk = own[0, i] + other[0, 0, i].astype(f32) * low + came[0, i].astype(f32)
            dn = unturn(dk, cos_ref[...], sin_ref[...])
            res[0, rows, :] = norm_back(dn, scr[rows, :], gain_ref[...])
            res[1, rows, :] = own[1, i] + other[0, 1, i].astype(f32) * low + came[1, i].astype(f32)
    kg_ref[...] = res[0].reshape(tokens, heads, width).astype(bf16)
    vg_ref[...] = res[1].reshape(tokens, heads, width).astype(bf16)


def params():
    return pltpu.CompilerParams(vmem_limit_bytes=VMEM_LIMIT)


def whole(kernel, outs, scratch, flops, bytes_accessed):
    return pl.pallas_call(
        kernel,
        out_shape=outs,
        scratch_shapes=scratch,
        compiler_params=params(),
        cost_estimate=pl.CostEstimate(
            flops=flops, bytes_accessed=bytes_accessed, transcendentals=0
        ),
    )


def body(queries, keys, values, output_gradient, window_start, query_gain, key_gain):
    tokens, heads, width = queries.shape
    groups = keys.shape[1]
    per = groups // CHUNKS
    reach = WINDOW_LENGTH // tokens
    span = WINDOW_LENGTH + HALF
    index = lax.axis_index("seq")
    core = lax.rem(index, 2)
    first = index * tokens
    low = core == 0
    positions = first - WINDOW_LENGTH + jnp.arange(WINDOW_LENGTH + tokens, dtype=jnp.int32)
    cos_all, sin_all = rope_tables(positions, width)
    cos_own, sin_own = rope_tables(first + jnp.arange(tokens, dtype=jnp.int32), width)
    sds = jax.ShapeDtypeStruct
    mib = 1 << 20

    own = list(whole(
        key_prep_kernel,
        [sds((2, per, tokens, width), bf16)] * CHUNKS,
        [pltpu.VMEM((2, tokens * groups, width), f32)],
        8 * mib, 2 * mib,
    )(keys, values, key_gain[None, :], cos_own, sin_own))
    near, far, side1, side3 = [], [], [], []
    for c in range(CHUNKS):
        near.append(hop(own[c], 2))
        far.append(hop(near[c], 2))
        side1.append(swap(jnp.where(low, own[c], near[c])))
        side3.append(swap(jnp.where(low, near[c], far[c])))

    starts = (window_start - first + WINDOW_LENGTH).reshape(tokens // HALF, HALF)
    qs, go, bias = whole(
        query_prep_kernel,
        [
            sds((groups, tokens // HALF, 2 * HALF, width), bf16),
            sds((groups, tokens // HALF, 2 * HALF, width), bf16),
            sds((tokens // HALF, span, HALF), f32),
        ],
        [pltpu.VMEM((2, tokens * heads, width), f32)],
        16 * mib, 5 * mib,
    )(queries, output_gradient, starts, query_gain[None, :], cos_own, sin_own)

    full = tokens * (reach + 1)
    kv_spec = pl.BlockSpec((2, 1, tokens, width), lambda i: (0, i, 0, 0))
    term_spec = pl.BlockSpec((2, 2, 1, tokens, width), lambda i: (0, 0, i, 0, 0))

    def at_rest(shape):
        return pl.BlockSpec(shape, lambda i: (0,) * len(shape))

    gains = jnp.zeros((2, width), f32)
    dqs, ends = [], []
    last = None
    for c in range(CHUNKS):
        if last is None:
            far[0], near[-1] = lax.optimization_barrier((far[0], near[-1]))
        else:
            own[c], last = lax.optimization_barrier((own[c], last))
        q_spec = pl.BlockSpec(
            (1, tokens // HALF, 2 * HALF, width), lambda i, c=c: (c * per + i, 0, 0, 0)
        )
        call = pl.pallas_call(
            main_kernel,
            grid=(per,),
            in_specs=[kv_spec] * 5
            + [q_spec] * 2
            + [
                at_rest((tokens // HALF, span, HALF)),
                at_rest((full, width)),
                at_rest((full, width)),
            ],
            out_specs=[
                term_spec,
                term_spec,
                kv_spec,
                pl.BlockSpec((1, tokens // HALF, 2 * HALF, width), lambda i: (i, 0, 0, 0)),
                at_rest((2, width)),
            ],
            out_shape=[
                sds((2, 2, per, tokens, width), bf16),
                sds((2, 2, per, tokens, width), bf16),
                sds((2, per, tokens, width), f32),
                sds((per, tokens // HALF, 2 * HALF, width), f32),
                sds((2, width), f32),
            ],
            scratch_shapes=[
                pltpu.VMEM((full, width), bf16),
                pltpu.VMEM((full, width), bf16),
                pltpu.VMEM((width, full), bf16),
                pltpu.VMEM((span, 2 * HALF), f32),
                pltpu.VMEM((span, 2 * HALF), f32),
                pltpu.VMEM((full, width), f32),
                pltpu.VMEM((full, width), f32),
            ],
            compiler_params=params(),
            cost_estimate=pl.CostEstimate(
                flops=2 * per * 2 * 5 * span * 2 * HALF * width * 2,
                bytes_accessed=per * 2 * mib,
                transcendentals=per * 2 * span * 2 * HALF,
            ),
            name="attention",
        )
        odd, even, mine, dq, gain = call(
            far[c], side3[c], near[c], side1[c], own[c], qs, go, bias, cos_all, sin_all
        )
        gains = gains + gain
        dqs.append(dq)
        other = swap(odd)
        send_far = even[0] + jnp.where(low, jnp.zeros_like(other[0]), other[0])
        came_far = hop(send_far, -2)
        send_near = even[1] + jnp.where(low, other[0], other[1]) + came_far
        ends += [mine, other, hop(send_near, -2)]
        last = send_far

    factor = jnp.stack([1.0 / (query_gain * query_scale), 1.0 / key_gain])
    gains = all_sum(gains * factor)

    call = whole(
        query_end_kernel,
        sds((tokens, heads, width), bf16),
        [pltpu.VMEM((tokens * heads, width), f32)] * 2,
        16 * mib, 4 * mib,
    )
    query_grad = call(queries, query_gain[None, :], *dqs)
    tile = 64
    token_spec = pl.BlockSpec((tile, groups, width), lambda i: (i, 0, 0))
    part_spec = pl.BlockSpec((2, per, tile, width), lambda i: (0, 0, i, 0))
    other_spec = pl.BlockSpec((1, 2, per, tile, width), lambda i: (1, 0, 0, i, 0))
    row_spec = pl.BlockSpec((tile, width), lambda i: (i, 0))
    key_grad, value_grad = pl.pallas_call(
        key_end_kernel,
        grid=(tokens // tile,),
        in_specs=[
            pl.BlockSpec(memory_space=pltpu.SMEM),
            token_spec,
            at_rest((1, width)),
            row_spec,
            row_spec,
        ]
        + [part_spec, other_spec, part_spec] * CHUNKS,
        out_specs=[token_spec] * 2,
        out_shape=[sds((tokens, groups, width), bf16)] * 2,
        scratch_shapes=[
            pltpu.VMEM((tile * groups, width), f32),
            pltpu.VMEM((2, tile * groups, width), f32),
        ],
        compiler_params=params(),
        cost_estimate=pl.CostEstimate(flops=8 * mib, bytes_accessed=4 * mib, transcendentals=0),
        name="key_end",
    )(low.astype(f32)[None], keys, key_gain[None, :], cos_own, sin_own, *ends)
    return query_grad, key_grad, value_grad, gains[0], gains[1]


def solution(mesh):
    wide = P("seq", "kv", None)
    return jax.shard_map(
        body,
        mesh=mesh,
        in_specs=(wide, wide, wide, wide, P("seq"), P(), P()),
        out_specs=(wide, wide, wide, P(), P()),
        check_vma=False,
    )
```

profile of v0, /device:TPU:24, one launch (start us, length us, event | category | flops | bytes accessed | tf_op | source)
XLA Modules:
  0.0 180.7 jit_solution(11419669725617061257)
XLA Ops:
  0.7 0.5 fusion.7
  1.2 0.8 pad_maximum_fusion.2
  2.0 3.6 %shard_map.110 = (bf16[2,4,256,128]{3,2,1,0:T(8,128)(2,1)}, bf16[2,4,256,128]{3,2,1,0:T(8,128)(2,1)}) custom-call(bf16[256,8,128]{2,1,0:T(8,128)(2,1)} %k_ref.3, bf16[256,8,128]{2,1,0:T(8,128)(2,1)} %v_ref.1, f32[1,128]{1,0:T(1,128)} %bitcast.27, f32[256,128]{1,0:T(8,128)} %get-tuple-element.57.cos_ref, f32[256,128]{1,0:T(8,128)} %get-tuple-element.58.sin_ref), custom_call_target="tpu_custom_call" | custom-call | flops 8388608 | bytes 2097152 | tf_op jit(solution)/shard_map/pallas_call | solution.py:266
  5.6 3.8 %collective-permute-start = (bf16[2,4,256,128]{3,2,1,0:T(8,128)(2,1)}, bf16[2,4,256,128]{3,2,1,0:T(8,128)(2,1)S(1)}, u32[]{:S(2)}, u32[]{:S(2)}) collective-permute-start(bf16[2,4,256,128]{3,2,1,0:T(8,128)(2,1)} %get-tuple-element.25.b0), channel_id=1, source_target_pairs={{0,4},{2,6},{4,8},{6,10},{8,12},{10,14},{12,16},{14,18},{16,20},{1... | collective-permute-start | bytes 1572872 | tf_op jit(solution)/shard_map/ppermute | solution.py:27
  9.4 18.7 %collective-permute-done.b2 = bf16[2,4,256,128]{3,2,1,0:T(8,128)(2,1)S(1)} collective-permute-done((bf16[2,4,256,128]{3,2,1,0:T(8,128)(2,1)}, bf16[2,4,256,128]{3,2,1,0:T(8,128)(2,1)S(1)}, u32[]{:S(2)}, u32[]{:S(2)}) %collective-permute-start) | collective-permute-done | bytes 524320 | tf_op jit(solution)/shard_map/ppermute | solution.py:27
  28.1 1.9 %collective-permute-start.1 = (bf16[2,4,256,128]{3,2,1,0:T(8,128)(2,1)S(1)}, bf16[2,4,256,128]{3,2,1,0:T(8,128)(2,1)S(1)}, u32[]{:S(2)}, u32[]{:S(2)}) collective-permute-start(bf16[2,4,256,128]{3,2,1,0:T(8,128)(2,1)S(1)} %collective-permute-done.b2), channel_id=1, source_target_pairs={{0,4},{2,6},{4,8},{6,10},{8,12},{10,14},{12,16},{14,18},{16,20},{1... | collective-permute-start | bytes 1572872 | tf_op jit(solution)/shard_map/ppermute | solution.py:27
  30.0 1.9 %collective-permute-start.2 = (bf16[2,4,256,128]{3,2,1,0:T(8,128)(2,1)}, bf16[2,4,256,128]{3,2,1,0:T(8,128)(2,1)S(1)}, u32[]{:S(2)}, u32[]{:S(2)}) collective-permute-start(bf16[2,4,256,128]{3,2,1,0:T(8,128)(2,1)} %get-tuple-element.35.b0), channel_id=1, source_target_pairs={{0,4},{2,6},{4,8},{6,10},{8,12},{10,14},{12,16},{14,18},{16,20},{1... | collective-permute-start | bytes 1572872 | tf_op jit(solution)/shard_map/ppermute | solution.py:27
  32.0 17.3 %collective-permute-done.1.b4 = bf16[2,4,256,128]{3,2,1,0:T(8,128)(2,1)S(1)} collective-permute-done((bf16[2,4,256,128]{3,2,1,0:T(8,128)(2,1)S(1)}, bf16[2,4,256,128]{3,2,1,0:T(8,128)(2,1)S(1)}, u32[]{:S(2)}, u32[]{:S(2)}) %collective-permute-start.1) | collective-permute-done | bytes 524320 | tf_op jit(solution)/shard_map/ppermute | solution.py:27
  49.3 2.4 %broadcast_select_fusion.2 = (bf16[2,4,256,128]{3,2,1,0:T(8,128)(2,1)}, bf16[2,4,256,128]{3,2,1,0:T(8,128)(2,1)}) fusion(bf16[2,4,256,128]{3,2,1,0:T(8,128)(2,1)} %get-tuple-element.25.b0, bf16[2,4,256,128]{3,2,1,0:T(8,128)(2,1)S(1)} %collective-permute-done.b2, pred[]{:T(512)S(6)} %eq.3, bf16[2,4,256,128]{3,2,1,0:T(8,128)(2,1)S(1)} %collective-permute-done.1.b4), kind=kLoop, calls=%fused_computation.16 | loop fusion | flops 524288 | bytes 2621441 | tf_op jit(solution)/shard_map/jit(_where)/select_n | solution.py:276
  51.8 0.5 collective-permute-start.4
  52.3 2.4 %fusion.6 = (f32[1280,64]{1,0:T(8,128)S(1)}, f32[1280,64]{1,0:T(8,128)S(1)}, f32[1280,64]{1,0:T(8,128)S(1)}) fusion(f32[64]{0:T(128)S(1)} %multiply_power_fusion, f32[1280]{0:T(1024)S(1)} %add_convert_fusion), kind=kLoop, calls=%fused_computation.18 | loop fusion | flops 163840 | bytes 988416 | tf_op jit(solution)/shard_map/neg | solution.py:53
  54.7 0.6 add_bitcast_fusion.2.start_ref
  55.3 6.9 %shard_map.111 = (bf16[8,2,256,128]{3,2,1,0:T(8,128)(2,1)}, bf16[8,2,256,128]{3,2,1,0:T(8,128)(2,1)}, f32[2,1152,128]{2,1,0:T(8,128)}) custom-call(bf16[256,16,128]{2,1,0:T(8,128)(2,1)} %q_ref.3, bf16[256,16,128]{2,1,0:T(8,128)(2,1)} %g_ref.1, s32[2,128]{1,0:T(2,128)} %add_bitcast_fusion.2.start_ref, f32[1,128]{1,0:T(1,128)} %bitcast.25, ...), custom_call_target="tpu_custom_call" | custom-call | flops 16777216 | bytes 5242880 | tf_op jit(solution)/shard_map/pallas_call | solution.py:280
  62.2 1.5 pad_maximum_fusion
  63.7 1.9 %collective-permute-start.5 = (bf16[2,4,256,128]{3,2,1,0:T(8,128)(2,1)S(1)}, bf16[2,4,256,128]{3,2,1,0:T(8,128)(2,1)S(1)}, u32[]{:S(2)}, u32[]{:S(2)}) collective-permute-start(bf16[2,4,256,128]{3,2,1,0:T(8,128)(2,1)S(1)} %collective-permute-done.2.b2), channel_id=1, source_target_pairs={{0,4},{2,6},{4,8},{6,10},{8,12},{10,14},{12,16},{14,18},{16,20},{1... | collective-permute-start | bytes 1572872 | tf_op jit(solution)/shard_map/ppermute | solution.py:27
  65.6 0.8 copy-done.15
  66.5 17.1 %attention.2 = (bf16[2,2,4,256,128]{4,3,2,1,0:T(8,128)(2,1)}, bf16[2,2,4,256,128]{4,3,2,1,0:T(8,128)(2,1)}, f32[2,4,256,128]{3,2,1,0:T(8,128)}, f32[4,2,256,128]{3,2,1,0:T(8,128)}, f32[2,128]{1,0:T(2,128)}) custom-call(bf16[2,4,256,128]{3,2,1,0:T(8,128)(2,1)} %copy-done.9, bf16[2,4,256,128]{3,2,1,0:T(8,128)(2,1)} %copy-done.15, ...), custom_call_target="tpu_custom_call" | custom-call | flops 6039797760 | bytes 8388608 | tf_op jit(solution)/shard_map/attention/pallas_call | solution.py:350
  83.7 0.3 collective-permute-done.5.b4
  84.1 0.7 copy-done.10
  84.9 0.4 collective-permute-start.7
  85.3 1.2 collective-permute-done.8.rest_1_
  86.5 0.9 add_bitcast_fusion.1
  87.4 0.6 collective-permute-done.7.b1
  88.0 0.3 copy-done.16
  88.3 0.8 copy-done.17
  89.1 17.1 %attention.3 = (bf16[2,2,4,256,128]{4,3,2,1,0:T(8,128)(2,1)}, bf16[2,2,4,256,128]{4,3,2,1,0:T(8,128)(2,1)}, f32[2,4,256,128]{3,2,1,0:T(8,128)}, f32[4,2,256,128]{3,2,1,0:T(8,128)}, f32[2,128]{1,0:T(2,128)}) custom-call(bf16[2,4,256,128]{3,2,1,0:T(8,128)(2,1)} %copy-done.10, bf16[2,4,256,128]{3,2,1,0:T(8,128)(2,1)} %copy-done.16, ...), custom_call_target="tpu_custom_call" | custom-call | flops 6039797760 | bytes 8388608 | tf_op jit(solution)/shard_map/attention/pallas_call | solution.py:350
  106.4 0.7 maximum_multiply_fusion
  107.1 0.4 collective-permute-start.14
  107.4 1.5 collective-permute-start.16
  108.9 8.4 %collective-permute-start.9 = (bf16[2,4,256,128]{3,2,1,0:T(8,128)(2,1)}, bf16[2,4,256,128]{3,2,1,0:T(8,128)(2,1)}, u32[]{:S(2)}, u32[]{:S(2)}) collective-permute-start(bf16[2,4,256,128]{3,2,1,0:T(8,128)(2,1)} %add_bitcast_fusion.1), channel_id=1, source_target_pairs={{4,0},{6,2},{8,4},{10,6},{12,8},{14,10},{16,12},{18,14},{20,16},{2... | collective-permute-start | bytes 1572872 | tf_op jit(solution)/shard_map/ppermute | solution.py:27
  117.4 2.3 %add_bitcast_fusion = bf16[2,4,256,128]{3,2,1,0:T(8,128)(2,1)} fusion(bf16[2,2,4,256,128]{4,3,2,1,0:T(8,128)(2,1)} %get-tuple-element.40, pred[]{:T(512)S(6)} %eq.3, bf16[2,2,4,256,128]{4,3,2,1,0:T(8,128)(2,1)S(1)} %collective-permute-done.11.rest_4_), kind=kLoop, calls=%fused_computation.12 | loop fusion | flops 524288 | bytes 1572865 | tf_op jit(solution)/shard_map/add | solution.py:356
  119.6 2.4 %collective-permute-start.12 = (bf16[2,4,256,128]{3,2,1,0:T(8,128)(2,1)}, bf16[2,4,256,128]{3,2,1,0:T(8,128)(2,1)}, u32[]{:S(2)}, u32[]{:S(2)}) collective-permute-start(bf16[2,4,256,128]{3,2,1,0:T(8,128)(2,1)} %add_bitcast_fusion), channel_id=1, source_target_pairs={{4,0},{6,2},{8,4},{10,6},{12,8},{14,10},{16,12},{18,14},{20,16},{2... | collective-permute-start | bytes 1572872 | tf_op jit(solution)/shard_map/ppermute | solution.py:27
  122.3 6.4 %collective-permute-start.19 = (f32[2,128]{1,0:T(2,128)S(1)}, f32[2,128]{1,0:T(2,128)S(1)}, u32[]{:S(2)}, u32[]{:S(2)}) collective-permute-start(f32[2,128]{1,0:T(2,128)S(1)} %add_add_fusion.3), channel_id=1, source_target_pairs={{0,24},{1,25},{2,26},{3,27},{4,28},{5,29},{6,30},{7,31},{8,16},{9,... | collective-permute-start | bytes 3080 | tf_op jit(solution)/shard_map/ppermute | solution.py:42
  128.7 7.6 %collective-permute-done.17 = f32[2,128]{1,0:T(2,128)S(1)} collective-permute-done((f32[2,128]{1,0:T(2,128)S(1)}, f32[2,128]{1,0:T(2,128)S(1)}, u32[]{:S(2)}, u32[]{:S(2)}) %collective-permute-start.17) | collective-permute-done | bytes 1056 | tf_op jit(solution)/shard_map/ppermute | solution.py:42
  136.3 4.7 %collective-permute-done.19 = f32[2,128]{1,0:T(2,128)S(1)} collective-permute-done((f32[2,128]{1,0:T(2,128)S(1)}, f32[2,128]{1,0:T(2,128)S(1)}, u32[]{:S(2)}, u32[]{:S(2)}) %collective-permute-start.19) | collective-permute-done | bytes 1056 | tf_op jit(solution)/shard_map/ppermute | solution.py:42
  141.0 0.6 collective-permute-start.20
  141.6 4.1 %collective-permute-start.22 = (f32[2,128]{1,0:T(2,128)S(1)}, f32[2,128]{1,0:T(2,128)S(1)}, u32[]{:S(2)}, u32[]{:S(2)}) collective-permute-start(f32[2,128]{1,0:T(2,128)S(1)} %add_add_fusion.2), channel_id=1, source_target_pairs={{0,33},{1,32},{2,35},{3,34},{4,37},{5,36},{6,39},{7,38},{8,41},{9,... | collective-permute-start | bytes 3080 | tf_op jit(solution)/shard_map/ppermute | solution.py:42
  145.7 1.9 %fusion.5 = bf16[2,4,256,128]{3,2,1,0:T(8,128)(2,1)} fusion(bf16[2,4,256,128]{3,2,1,0:T(8,128)(2,1)} %collective-permute-done.9, bf16[2,2,4,256,128]{4,3,2,1,0:T(8,128)(2,1)S(1)} %collective-permute-done.8.rest_1_, bf16[2,2,4,256,128]{4,3,2,1,0:T(8,128)(2,1)S(1)} %copy-done.2, pred[]{:T(512)S(6)} %eq.3), kind=kLoop, calls=%fused_computation.11 | loop fusion | flops 786432 | bytes 2621441 | tf_op jit(solution)/shard_map/add | solution.py:358
  147.6 1.9 %collective-permute-start.10 = (bf16[2,4,256,128]{3,2,1,0:T(8,128)(2,1)}, bf16[2,4,256,128]{3,2,1,0:T(8,128)(2,1)S(1)}, u32[]{:S(2)}, u32[]{:S(2)}) collective-permute-start(bf16[2,4,256,128]{3,2,1,0:T(8,128)(2,1)} %fusion.5), channel_id=1, source_target_pairs={{4,0},{6,2},{8,4},{10,6},{12,8},{14,10},{16,12},{18,14},{20,16},{2... | collective-permute-start | bytes 1572872 | tf_op jit(solution)/shard_map/ppermute | solution.py:27
  149.5 1.1 fusion.2
  150.7 5.7 %collective-permute-start.13 = (bf16[2,4,256,128]{3,2,1,0:T(8,128)(2,1)S(1)}, bf16[2,4,256,128]{3,2,1,0:T(8,128)(2,1)S(1)}, u32[]{:S(2)}, u32[]{:S(2)}) collective-permute-start(bf16[2,4,256,128]{3,2,1,0:T(8,128)(2,1)S(1)} %fusion.2), channel_id=1, source_target_pairs={{4,0},{6,2},{8,4},{10,6},{12,8},{14,10},{16,12},{18,14},{20,16},{2... | collective-permute-start | bytes 1572872 | tf_op jit(solution)/shard_map/ppermute | solution.py:27
  156.5 0.5 collective-permute-start.23
  157.0 4.2 %collective-permute-start.25 = (f32[2,128]{1,0:T(2,128)S(1)}, f32[2,128]{1,0:T(2,128)S(1)}, u32[]{:S(2)}, u32[]{:S(2)}) collective-permute-start(f32[2,128]{1,0:T(2,128)S(1)} %add_add_fusion.1), channel_id=1, source_target_pairs={{0,192},{1,193},{2,194},{3,195},{4,196},{5,197},{6,198},{7,199},{8... | collective-permute-start | bytes 3080 | tf_op jit(solution)/shard_map/ppermute | solution.py:42
  161.2 6.0 %shard_map.112 = bf16[256,16,128]{2,1,0:T(8,128)(2,1)} custom-call(bf16[256,16,128]{2,1,0:T(8,128)(2,1)} %q_ref.3, f32[1,128]{1,0:T(1,128)} %bitcast.26, f32[4,2,256,128]{3,2,1,0:T(8,128)} %get-tuple-element.31.rest_0_, f32[4,2,256,128]{3,2,1,0:T(8,128)} %get-tuple-element.36.rest_1_), custom_call_target="tpu_custom_call" | custom-call | flops 16777216 | bytes 4194304 | tf_op jit(solution)/shard_map/pallas_call | solution.py:371
  167.3 0.5 slice_bitcast_fusion
  167.8 5.9 %collective-permute-done.13.rest_5_ = bf16[2,4,256,128]{3,2,1,0:T(8,128)(2,1)S(1)} collective-permute-done((bf16[2,4,256,128]{3,2,1,0:T(8,128)(2,1)S(1)}, bf16[2,4,256,128]{3,2,1,0:T(8,128)(2,1)S(1)}, u32[]{:S(2)}, u32[]{:S(2)}) %collective-permute-start.13) | collective-permute-done | bytes 524320 | tf_op jit(solution)/shard_map/ppermute | solution.py:27
  173.7 0.8 copy-done.5
  174.5 6.0 %key_end.1 = (bf16[256,8,128]{2,1,0:T(8,128)(2,1)}, bf16[256,8,128]{2,1,0:T(8,128)(2,1)}) custom-call(f32[1]{0:T(128)} %bitcast.4.low_ref, bf16[256,8,128]{2,1,0:T(8,128)(2,1)} %k_ref.3, f32[1,128]{1,0:T(1,128)} %bitcast.28, f32[256,128]{1,0:T(8,128)} %get-tuple-element.57.cos_ref, f32[256,128]{1,0:T(8,128)} %get-tuple-element.58.sin_ref, ...), custom_call_target="tpu_custom_call" | custom-call | flops 8388608 | bytes 4194304 | tf_op jit(solution)/shard_map/key_end/pallas_call | solution.py:377
  (68 shorter events, 1.1 us)
Async XLA Ops:
  5.6 22.5 %collective-permute-start = (bf16[2,4,256,128]{3,2,1,0:T(8,128)(2,1)}, bf16[2,4,256,128]{3,2,1,0:T(8,128)(2,1)S(1)}, u32[]{:S(2)}, u32[]{:S(2)}) collective-permute-start(bf16[2,4,256,128]{3,2,1,0:T(8,128)(2,1)} %get-tuple-element.25.b0), channel_id=1, source_target_pairs={{0,4},{2,6},{4,8},{6,10},{8,12},{10,14},{12,16},{14,18},{16,20},{1... | collective-permute-start | bytes 1572872 | tf_op jit(solution)/shard_map/ppermute | solution.py:27
  28.1 23.6 %copy-start.8 = (bf16[2,4,256,128]{3,2,1,0:T(8,128)(2,1)}, bf16[2,4,256,128]{3,2,1,0:T(8,128)(2,1)S(1)}, u32[]{:S(2)}) copy-start(bf16[2,4,256,128]{3,2,1,0:T(8,128)(2,1)S(1)} %collective-permute-done.b2) | copy-start | bytes 1572868
  28.1 21.2 %collective-permute-start.1 = (bf16[2,4,256,128]{3,2,1,0:T(8,128)(2,1)S(1)}, bf16[2,4,256,128]{3,2,1,0:T(8,128)(2,1)S(1)}, u32[]{:S(2)}, u32[]{:S(2)}) collective-permute-start(bf16[2,4,256,128]{3,2,1,0:T(8,128)(2,1)S(1)} %collective-permute-done.b2), channel_id=1, source_target_pairs={{0,4},{2,6},{4,8},{6,10},{8,12},{10,14},{12,16},{14,18},{16,20},{1... | collective-permute-start | bytes 1572872 | tf_op jit(solution)/shard_map/ppermute | solution.py:27
  30.0 33.6 %collective-permute-start.2 = (bf16[2,4,256,128]{3,2,1,0:T(8,128)(2,1)}, bf16[2,4,256,128]{3,2,1,0:T(8,128)(2,1)S(1)}, u32[]{:S(2)}, u32[]{:S(2)}) collective-permute-start(bf16[2,4,256,128]{3,2,1,0:T(8,128)(2,1)} %get-tuple-element.35.b0), channel_id=1, source_target_pairs={{0,4},{2,6},{4,8},{6,10},{8,12},{10,14},{12,16},{14,18},{16,20},{1... | collective-permute-start | bytes 1572872 | tf_op jit(solution)/shard_map/ppermute | solution.py:27
  49.3 2.4 %copy-start.9 = (bf16[2,4,256,128]{3,2,1,0:T(8,128)(2,1)}, bf16[2,4,256,128]{3,2,1,0:T(8,128)(2,1)S(1)}, u32[]{:S(2)}) copy-start(bf16[2,4,256,128]{3,2,1,0:T(8,128)(2,1)S(1)} %collective-permute-done.1.b4) | copy-start | bytes 1572868
  51.7 3.0 %copy-start.13 = (s32[256]{0:T(256)S(1)}, s32[256]{0:T(256)}, u32[]{:S(2)}) copy-start(s32[256]{0:T(256)} %param.11) | copy-start | bytes 3076
  51.7 13.9 %collective-permute-start.3 = (bf16[2,4,256,128]{3,2,1,0:T(8,128)(2,1)}, bf16[2,4,256,128]{3,2,1,0:T(8,128)(2,1)S(1)}, u32[]{:S(2)}, u32[]{:S(2)}) collective-permute-start(bf16[2,4,256,128]{3,2,1,0:T(8,128)(2,1)} %get-tuple-element.48), channel_id=1, source_target_pairs={{0,2},{2,0},{4,6},{6,4},{8,10},{10,8},{12,14},{14,12},{16,18},{18,... | collective-permute-start | bytes 1572872 | tf_op jit(solution)/shard_map/ppermute | solution.py:31
  51.8 13.8 %collective-permute-start.4 = (bf16[2,4,256,128]{3,2,1,0:T(8,128)(2,1)}, bf16[2,4,256,128]{3,2,1,0:T(8,128)(2,1)}, u32[]{:S(2)}, u32[]{:S(2)}) collective-permute-start(bf16[2,4,256,128]{3,2,1,0:T(8,128)(2,1)} %get-tuple-element.47), channel_id=1, source_target_pairs={{0,2},{2,0},{4,6},{6,4},{8,10},{10,8},{12,14},{14,12},{16,18},{18,... | collective-permute-start | bytes 1572872 | tf_op jit(solution)/shard_map/ppermute | solution.py:31
  63.7 20.3 %copy-start.7 = (bf16[2,4,256,128]{3,2,1,0:T(8,128)(2,1)}, bf16[2,4,256,128]{3,2,1,0:T(8,128)(2,1)S(1)}, u32[]{:S(2)}) copy-start(bf16[2,4,256,128]{3,2,1,0:T(8,128)(2,1)S(1)} %collective-permute-done.2.b2) | copy-start | bytes 1572868
  63.7 20.3 %collective-permute-start.5 = (bf16[2,4,256,128]{3,2,1,0:T(8,128)(2,1)S(1)}, bf16[2,4,256,128]{3,2,1,0:T(8,128)(2,1)S(1)}, u32[]{:S(2)}, u32[]{:S(2)}) collective-permute-start(bf16[2,4,256,128]{3,2,1,0:T(8,128)(2,1)S(1)} %collective-permute-done.2.b2), channel_id=1, source_target_pairs={{0,4},{2,6},{4,8},{6,10},{8,12},{10,14},{12,16},{14,18},{16,20},{1... | collective-permute-start | bytes 1572872 | tf_op jit(solution)/shard_map/ppermute | solution.py:27
  65.6 0.9 copy-start.15
  66.5 17.5 %copy-start.6 = (bf16[2,4,256,128]{3,2,1,0:T(8,128)(2,1)S(1)}, bf16[2,4,256,128]{3,2,1,0:T(8,128)(2,1)}, u32[]{:S(2)}) copy-start(bf16[2,4,256,128]{3,2,1,0:T(8,128)(2,1)} %get-tuple-element.35.b0) | copy-start | bytes 1572868
  83.5 3.0 %copy-start.2 = (bf16[2,2,4,256,128]{4,3,2,1,0:T(8,128)(2,1)S(1)}, bf16[2,2,4,256,128]{4,3,2,1,0:T(8,128)(2,1)}, u32[]{:S(2)}) copy-start(bf16[2,2,4,256,128]{4,3,2,1,0:T(8,128)(2,1)} %get-tuple-element.33) | copy-start | bytes 3145732
  83.5 3.0 %collective-permute-start.8 = (bf16[2,2,4,256,128]{4,3,2,1,0:T(8,128)(2,1)}, bf16[2,2,4,256,128]{4,3,2,1,0:T(8,128)(2,1)S(1)}, u32[]{:S(2)}, u32[]{:S(2)}) collective-permute-start(bf16[2,2,4,256,128]{4,3,2,1,0:T(8,128)(2,1)} %get-tuple-element.34), channel_id=1, source_target_pairs={{0,2},{2,0},{4,6},{6,4},{8,10},{10,8},{12,14},{14,12},{16,18},{18,... | collective-permute-start | bytes 3145736 | tf_op jit(solution)/shard_map/ppermute | solution.py:31
  84.0 0.8 copy-start.10
  84.8 2.6 %collective-permute-start.6 = (bf16[2,4,256,128]{3,2,1,0:T(8,128)(2,1)S(1)}, bf16[2,4,256,128]{3,2,1,0:T(8,128)(2,1)S(1)}, u32[]{:S(2)}, u32[]{:S(2)}) collective-permute-start(bf16[2,4,256,128]{3,2,1,0:T(8,128)(2,1)S(1)} %get-tuple-element.46), channel_id=1, source_target_pairs={{0,2},{2,0},{4,6},{6,4},{8,10},{10,8},{12,14},{14,12},{16,18},{18,... | collective-permute-start | bytes 1572872 | tf_op jit(solution)/shard_map/ppermute | solution.py:31
  84.9 3.1 %collective-permute-start.7 = (bf16[2,4,256,128]{3,2,1,0:T(8,128)(2,1)S(1)}, bf16[2,4,256,128]{3,2,1,0:T(8,128)(2,1)S(1)}, u32[]{:S(2)}, u32[]{:S(2)}) collective-permute-start(bf16[2,4,256,128]{3,2,1,0:T(8,128)(2,1)S(1)} %get-tuple-element.45), channel_id=1, source_target_pairs={{0,2},{2,0},{4,6},{6,4},{8,10},{10,8},{12,14},{14,12},{16,18},{18,... | collective-permute-start | bytes 1572872 | tf_op jit(solution)/shard_map/ppermute | solution.py:31
  86.5 59.2 %copy-start = (bf16[2,2,4,256,128]{4,3,2,1,0:T(8,128)(2,1)}, bf16[2,2,4,256,128]{4,3,2,1,0:T(8,128)(2,1)S(1)}, u32[]{:S(2)}) copy-start(bf16[2,2,4,256,128]{4,3,2,1,0:T(8,128)(2,1)S(1)} %collective-permute-done.8.rest_1_) | copy-start | bytes 3145732
  87.4 18.9 %copy-start.12 = (f32[128]{0:T(128)S(1)}, f32[128]{0:T(128)}, u32[]{:S(2)}) copy-start(f32[128]{0:T(128)} %param.13) | copy-start | bytes 1540
  87.4 18.9 %copy-start.11 = (f32[128]{0:T(128)S(1)}, f32[128]{0:T(128)}, u32[]{:S(2)}) copy-start(f32[128]{0:T(128)} %param.12) | copy-start | bytes 1540
  87.4 19.0 %copy-start.14 = (f32[2,128]{1,0:T(2,128)S(1)}, f32[2,128]{1,0:T(2,128)}, u32[]{:S(2)}) copy-start(f32[2,128]{1,0:T(2,128)} %get-tuple-element.43) | copy-start | bytes 3076
  87.4 0.8 copy-start.16
  88.2 0.8 copy-start.17
  106.1 11.2 %collective-permute-start.11 = (bf16[2,2,4,256,128]{4,3,2,1,0:T(8,128)(2,1)}, bf16[2,2,4,256,128]{4,3,2,1,0:T(8,128)(2,1)S(1)}, u32[]{:S(2)}, u32[]{:S(2)}) collective-permute-start(bf16[2,2,4,256,128]{4,3,2,1,0:T(8,128)(2,1)} %get-tuple-element.39), channel_id=1, source_target_pairs={{0,2},{2,0},{4,6},{6,4},{8,10},{10,8},{12,14},{14,12},{16,18},{18,... | collective-permute-start | bytes 3145736 | tf_op jit(solution)/shard_map/ppermute | solution.py:31
  107.1 15.0 %collective-permute-start.14 = (f32[2,128]{1,0:T(2,128)S(1)}, f32[2,128]{1,0:T(2,128)S(1)}, u32[]{:S(2)}, u32[]{:S(2)}) collective-permute-start(f32[2,128]{1,0:T(2,128)S(1)} %maximum_multiply_fusion), channel_id=1, source_target_pairs={{0,2},{1,3},{2,0},{3,1},{4,6},{5,7},{6,4},{7,5},{8,10},{9,11},{10,... | collective-permute-start | bytes 3080 | tf_op jit(solution)/shard_map/ppermute | solution.py:42
  107.4 14.7 %collective-permute-start.15 = (f32[2,128]{1,0:T(2,128)S(1)}, f32[2,128]{1,0:T(2,128)S(1)}, u32[]{:S(2)}, u32[]{:S(2)}) collective-permute-start(f32[2,128]{1,0:T(2,128)S(1)} %maximum_multiply_fusion), channel_id=1, source_target_pairs={{0,4},{1,5},{2,6},{3,7},{4,0},{5,1},{6,2},{7,3},{8,12},{9,13},{10,... | collective-permute-start | bytes 3080 | tf_op jit(solution)/shard_map/ppermute | solution.py:42
  107.4 14.7 %collective-permute-start.16 = (f32[2,128]{1,0:T(2,128)S(1)}, f32[2,128]{1,0:T(2,128)S(1)}, u32[]{:S(2)}, u32[]{:S(2)}) collective-permute-start(f32[2,128]{1,0:T(2,128)S(1)} %maximum_multiply_fusion), channel_id=1, source_target_pairs={{0,6},{1,7},{2,4},{3,5},{4,2},{5,3},{6,0},{7,1},{8,14},{9,15},{10,... | collective-permute-start | bytes 3080 | tf_op jit(solution)/shard_map/ppermute | solution.py:42
  108.9 36.7 %collective-permute-start.9 = (bf16[2,4,256,128]{3,2,1,0:T(8,128)(2,1)}, bf16[2,4,256,128]{3,2,1,0:T(8,128)(2,1)}, u32[]{:S(2)}, u32[]{:S(2)}) collective-permute-start(bf16[2,4,256,128]{3,2,1,0:T(8,128)(2,1)} %add_bitcast_fusion.1), channel_id=1, source_target_pairs={{4,0},{6,2},{8,4},{10,6},{12,8},{14,10},{16,12},{18,14},{20,16},{2... | collective-permute-start | bytes 1572872 | tf_op jit(solution)/shard_map/ppermute | solution.py:27
  117.4 32.2 %copy-start.1 = (bf16[2,2,4,256,128]{4,3,2,1,0:T(8,128)(2,1)}, bf16[2,2,4,256,128]{4,3,2,1,0:T(8,128)(2,1)S(1)}, u32[]{:S(2)}) copy-start(bf16[2,2,4,256,128]{4,3,2,1,0:T(8,128)(2,1)S(1)} %collective-permute-done.11.rest_4_) | copy-start | bytes 3145732
  119.6 29.9 %collective-permute-start.12 = (bf16[2,4,256,128]{3,2,1,0:T(8,128)(2,1)}, bf16[2,4,256,128]{3,2,1,0:T(8,128)(2,1)}, u32[]{:S(2)}, u32[]{:S(2)}) collective-permute-start(bf16[2,4,256,128]{3,2,1,0:T(8,128)(2,1)} %add_bitcast_fusion), channel_id=1, source_target_pairs={{4,0},{6,2},{8,4},{10,6},{12,8},{14,10},{16,12},{18,14},{20,16},{2... | collective-permute-start | bytes 1572872 | tf_op jit(solution)/shard_map/ppermute | solution.py:27
  122.1 14.1 %collective-permute-start.17 = (f32[2,128]{1,0:T(2,128)S(1)}, f32[2,128]{1,0:T(2,128)S(1)}, u32[]{:S(2)}, u32[]{:S(2)}) collective-permute-start(f32[2,128]{1,0:T(2,128)S(1)} %add_add_fusion.3), channel_id=1, source_target_pairs={{0,8},{1,9},{2,10},{3,11},{4,12},{5,13},{6,14},{7,15},{8,0},{9,1},... | collective-permute-start | bytes 3080 | tf_op jit(solution)/shard_map/ppermute | solution.py:42
  122.2 14.0 %collective-permute-start.18 = (f32[2,128]{1,0:T(2,128)S(1)}, f32[2,128]{1,0:T(2,128)S(1)}, u32[]{:S(2)}, u32[]{:S(2)}) collective-permute-start(f32[2,128]{1,0:T(2,128)S(1)} %add_add_fusion.3), channel_id=1, source_target_pairs={{0,16},{1,17},{2,18},{3,19},{4,20},{5,21},{6,22},{7,23},{8,24},{9,... | collective-permute-start | bytes 3080 | tf_op jit(solution)/shard_map/ppermute | solution.py:42
  122.3 18.6 %collective-permute-start.19 = (f32[2,128]{1,0:T(2,128)S(1)}, f32[2,128]{1,0:T(2,128)S(1)}, u32[]{:S(2)}, u32[]{:S(2)}) collective-permute-start(f32[2,128]{1,0:T(2,128)S(1)} %add_add_fusion.3), channel_id=1, source_target_pairs={{0,24},{1,25},{2,26},{3,27},{4,28},{5,29},{6,30},{7,31},{8,16},{9,... | collective-permute-start | bytes 3080 | tf_op jit(solution)/shard_map/ppermute | solution.py:42
  141.0 8.6 %copy-start.3 = (bf16[2,2,4,256,128]{4,3,2,1,0:T(8,128)(2,1)S(1)}, bf16[2,2,4,256,128]{4,3,2,1,0:T(8,128)(2,1)}, u32[]{:S(2)}) copy-start(bf16[2,2,4,256,128]{4,3,2,1,0:T(8,128)(2,1)} %get-tuple-element.40) | copy-start | bytes 3145732
  141.0 15.5 %collective-permute-start.20 = (f32[2,128]{1,0:T(2,128)S(1)}, f32[2,128]{1,0:T(2,128)S(1)}, u32[]{:S(2)}, u32[]{:S(2)}) collective-permute-start(f32[2,128]{1,0:T(2,128)S(1)} %add_add_fusion.2), channel_id=1, source_target_pairs={{0,1},{1,0},{2,3},{3,2},{4,5},{5,4},{6,7},{7,6},{8,9},{9,8},{10,11... | collective-permute-start | bytes 3080 | tf_op jit(solution)/shard_map/ppermute | solution.py:42
  141.6 14.9 %collective-permute-start.21 = (f32[2,128]{1,0:T(2,128)S(1)}, f32[2,128]{1,0:T(2,128)S(1)}, u32[]{:S(2)}, u32[]{:S(2)}) collective-permute-start(f32[2,128]{1,0:T(2,128)S(1)} %add_add_fusion.2), channel_id=1, source_target_pairs={{0,32},{1,33},{2,34},{3,35},{4,36},{5,37},{6,38},{7,39},{8,40},{9,... | collective-permute-start | bytes 3080 | tf_op jit(solution)/shard_map/ppermute | solution.py:42
  141.6 14.8 %collective-permute-start.22 = (f32[2,128]{1,0:T(2,128)S(1)}, f32[2,128]{1,0:T(2,128)S(1)}, u32[]{:S(2)}, u32[]{:S(2)}) collective-permute-start(f32[2,128]{1,0:T(2,128)S(1)} %add_add_fusion.2), channel_id=1, source_target_pairs={{0,33},{1,32},{2,35},{3,34},{4,37},{5,36},{6,39},{7,38},{8,41},{9,... | collective-permute-start | bytes 3080 | tf_op jit(solution)/shard_map/ppermute | solution.py:42
  147.6 20.2 %collective-permute-start.10 = (bf16[2,4,256,128]{3,2,1,0:T(8,128)(2,1)}, bf16[2,4,256,128]{3,2,1,0:T(8,128)(2,1)S(1)}, u32[]{:S(2)}, u32[]{:S(2)}) collective-permute-start(bf16[2,4,256,128]{3,2,1,0:T(8,128)(2,1)} %fusion.5), channel_id=1, source_target_pairs={{4,0},{6,2},{8,4},{10,6},{12,8},{14,10},{16,12},{18,14},{20,16},{2... | collective-permute-start | bytes 1572872 | tf_op jit(solution)/shard_map/ppermute | solution.py:27
  150.7 23.0 %collective-permute-start.13 = (bf16[2,4,256,128]{3,2,1,0:T(8,128)(2,1)S(1)}, bf16[2,4,256,128]{3,2,1,0:T(8,128)(2,1)S(1)}, u32[]{:S(2)}, u32[]{:S(2)}) collective-permute-start(bf16[2,4,256,128]{3,2,1,0:T(8,128)(2,1)S(1)} %fusion.2), channel_id=1, source_target_pairs={{4,0},{6,2},{8,4},{10,6},{12,8},{14,10},{16,12},{18,14},{20,16},{2... | collective-permute-start | bytes 1572872 | tf_op jit(solution)/shard_map/ppermute | solution.py:27
  156.5 10.8 %collective-permute-start.23 = (f32[2,128]{1,0:T(2,128)S(1)}, f32[2,128]{1,0:T(2,128)S(1)}, u32[]{:S(2)}, u32[]{:S(2)}) collective-permute-start(f32[2,128]{1,0:T(2,128)S(1)} %add_add_fusion.1), channel_id=1, source_target_pairs={{0,64},{1,65},{2,66},{3,67},{4,68},{5,69},{6,70},{7,71},{8,72},{9,... | collective-permute-start | bytes 3080 | tf_op jit(solution)/shard_map/ppermute | solution.py:42
  157.0 10.3 %collective-permute-start.24 = (f32[2,128]{1,0:T(2,128)S(1)}, f32[2,128]{1,0:T(2,128)S(1)}, u32[]{:S(2)}, u32[]{:S(2)}) collective-permute-start(f32[2,128]{1,0:T(2,128)S(1)} %add_add_fusion.1), channel_id=1, source_target_pairs={{0,128},{1,129},{2,130},{3,131},{4,132},{5,133},{6,134},{7,135},{8... | collective-permute-start | bytes 3080 | tf_op jit(solution)/shard_map/ppermute | solution.py:42
  157.0 10.3 %collective-permute-start.25 = (f32[2,128]{1,0:T(2,128)S(1)}, f32[2,128]{1,0:T(2,128)S(1)}, u32[]{:S(2)}, u32[]{:S(2)}) collective-permute-start(f32[2,128]{1,0:T(2,128)S(1)} %add_add_fusion.1), channel_id=1, source_target_pairs={{0,192},{1,193},{2,194},{3,195},{4,196},{5,197},{6,198},{7,199},{8... | collective-permute-start | bytes 3080 | tf_op jit(solution)/shard_map/ppermute | solution.py:42
  167.8 5.9 %copy-start.4 = (bf16[2,4,256,128]{3,2,1,0:T(8,128)(2,1)}, bf16[2,4,256,128]{3,2,1,0:T(8,128)(2,1)S(1)}, u32[]{:S(2)}) copy-start(bf16[2,4,256,128]{3,2,1,0:T(8,128)(2,1)S(1)} %collective-permute-done.10.rest_2_) | copy-start | bytes 1572868
  173.7 0.8 copy-start.5
where the time goes:
time: 181 us
  Pallas kernels  56.7 us (31%)
  waiting for transfers between devices  56.2 us (31%)
  starting transfers between devices  47.4 us (26%)
  other arithmetic  15.3 us (8%)
  local copies, waits for them, and re-layouts  3.99 us (2%)
    ppermute x8, waiting for transfers between devices, hop(): lax.ppermute(value, 'seq', [(s, s + steps) for s in range(first, last)])  42.1 us
    pallas_call x2, Pallas kernels, body(): call(far[c], side3[c], near[c], side1[c], own[c], qs, go, bias, cos_all,...  34.1 us
    ppermute x8, starting transfers between devices, hop(): lax.ppermute(value, 'seq', [(s, s + steps) for s in range(first, last)])  28 us
    ppermute x12, starting transfers between devices, all_sum(): lax.ppermute(value, ('seq', 'kv'), [(s, s ^ m) for s in range(count)])  17.9 us
    ppermute x12, waiting for transfers between devices, all_sum(): lax.ppermute(value, ('seq', 'kv'), [(s, s ^ m) for s in range(count)])  12.3 us
    pallas_call x1, Pallas kernels, body(): whole(query_prep_kernel, [sds((groups, tokens // HALF, 2 * HALF, width),...  6.91 us
    pallas_call x1, Pallas kernels, body(): pl.pallas_call(key_end_kernel, grid=(tokens // tile,), in_specs=[pl.Block...  6.05 us
    pallas_call x1, Pallas kernels, body(): query_grad = call(queries, query_gain[None, :], *dqs)  6.05 us
  transfers between devices with their start and end apart: 26, of which 8 were waited for; matrix products, arithmetic and copies ran while one was open for 8% of the time, Pallas kernels for 17%

commit v1 on v0

v1 whole, which is shorter than its diff:
```python
import functools
import math

import jax
import jax.numpy as jnp
import numpy as np
from jax import lax
from jax.experimental import pallas as pl
from jax.experimental.pallas import tpu as pltpu
from jax.sharding import PartitionSpec as P


WINDOW_LENGTH = 1024
SPLIT = (4, 4)
TILE = 64
attn_scale = 168.0 ** (-0.5)
norm_eps = 1e-06
rope_base = 10000.0
query_scale = attn_scale * math.log2(math.e)
VMEM_LIMIT = 60 * 1024 * 1024
HALF = 128
bf16 = jnp.bfloat16
f32 = jnp.float32


def hop(value, steps):
    count = lax.axis_size("seq")
    first, last = max(0, -steps), min(count, count - steps)
    return lax.ppermute(value, "seq", [(s, s + steps) for s in range(first, last)])


def swap(value, cores=(0, 1)):
    pairs = [(s, s ^ 1) for s in range(lax.axis_size("seq")) if s % 2 in cores]
    return lax.ppermute(value, "seq", pairs)


def sum_rounds(count):
    if count != 256:
        return [[[s ^ (1 << i) for s in range(count)]] for i in range(count.bit_length() - 1)]

    def flip(*masks):
        return [[s ^ m for s in range(count)] for m in masks]

    def ahead(steps):
        return [(s & ~28) | (((s >> 2) + steps) % 8 << 2) for s in range(count)]

    return [flip(1, 2, 3), [ahead(1), ahead(2), ahead(3)], flip(64, 128, 192), flip(16, 32, 48)]


def all_sum(value):
    count = lax.axis_size("seq") * lax.axis_size("kv")
    for targets in sum_rounds(count):
        parts = [lax.ppermute(value, ("seq", "kv"), list(enumerate(target))) for target in targets]
        value = functools.reduce(lambda a, b: a + b, parts, value)
    return value


def rope_tables(positions, width):
    half = width // 2
    lane = lax.rem(jnp.arange(width, dtype=jnp.int32), half).astype(f32)
    sign = jnp.where(jnp.arange(width) < half, -1.0, 1.0).astype(f32)
    frequency = rope_base ** (-(lane * 2.0) / width)
    angles = positions.astype(f32)[:, None] * frequency[None, :]
    return jnp.cos(angles), jnp.sin(angles) * sign


def shift_table(tokens, reach, width):
    lane = np.arange(width) % (width // 2)
    sign = np.where(np.arange(width) < width // 2, -1.0, 1.0)
    angle = tokens * np.arange(reach, -1, -1.0)[:, None] * rope_base ** (-2.0 * lane / width)
    table = np.stack([np.cos(angle), np.sin(angle) * sign], 1)
    return table.reshape(2 * (reach + 1), width).astype(np.float32)


def turn(x, cos, sin):
    return x * cos + pltpu.roll(x, 64, 1) * sin


def unturn(x, cos, sin):
    return x * cos - pltpu.roll(x, 64, 1) * sin


def key_prep_kernel(k_ref, v_ref, gain_ref, cos_ref, sin_ref, *rest):
    out_refs, scr = rest[:-1], rest[-1]
    tokens, heads, width = k_ref.shape
    scr[0] = k_ref[...].astype(f32).reshape(tokens * heads, width)
    scr[1] = v_ref[...].astype(f32).reshape(tokens * heads, width)
    head = 0
    for out in out_refs:
        for i in range(out.shape[1]):
            x = scr[0, pl.ds(head, tokens, stride=heads), :]
            inv = lax.rsqrt(jnp.mean(x * x, axis=-1, keepdims=True) + norm_eps)
            x = x * inv * gain_ref[...]
            out[0, i] = turn(x, cos_ref[...], sin_ref[...]).astype(bf16)
            out[1, i] = scr[1, pl.ds(head, tokens, stride=heads), :].astype(bf16)
            head += 1


def query_prep_kernel(q_ref, g_ref, start_ref, gain_ref, cos_ref, sin_ref, qs_ref, go_ref, bias_ref, scr):
    tokens, heads, width = q_ref.shape
    scr[0] = q_ref[...].astype(f32).reshape(tokens * heads, width)
    scr[1] = g_ref[...].astype(f32).reshape(tokens * heads, width)
    for group in range(heads // 2):
        for r in range(2):
            rows = pl.ds(2 * group + r, tokens, stride=heads)
            x = scr[0, rows, :]
            inv = lax.rsqrt(jnp.mean(x * x, axis=-1, keepdims=True) + norm_eps) * query_scale
            x = x * inv * gain_ref[...]
            qs_ref[group, 0, r] = turn(x, cos_ref[...], sin_ref[...]).astype(bf16)
            go_ref[group, 0, r] = scr[1, rows, :].astype(bf16)
    step = pl.program_id(0)
    per = HALF // tokens

    @pl.when(lax.rem(step, per) == 0)
    def _():
        offset = lax.div(step, per) * HALF
        shape = bias_ref.shape[1:]
        key = lax.broadcasted_iota(jnp.int32, shape, 0) + offset
        token = lax.broadcasted_iota(jnp.int32, shape, 1) + offset
        seen = (key >= start_ref[0]) & (key <= token + WINDOW_LENGTH)
        bias_ref[0] = jnp.where(seen, 0.0, -1e30).astype(f32)


NT = (((1,), (1,)), ((), ()))


def dot(a, b, dims=(((1,), (0,)), ((), ()))):
    return lax.dot_general(a, b, dims, preferred_element_type=f32)


def turned_sum(same, cross, cos, sin):
    kept = jnp.sum(same * cos * cos, axis=0, keepdims=True)
    moved = jnp.sum(same * sin * sin, axis=0, keepdims=True)
    mixed = jnp.sum(cross * cos * sin, axis=0, keepdims=True)
    return kept - mixed + pltpu.roll(moved + mixed, 64, 1)


def main_kernel(
    low_ref, far, near, own, side_own, side_near, side_far, q_ref, g_ref, bias_ref, cos_ref, sin_ref, shift_ref,
    odd_ref, even_ref, own_ref, dq_ref, gain_ref,
    k_scr, v_scr, kt_scr, e_scr, p_scr, ks_scr, kx_scr, qs_scr, qx_scr,
):
    tokens, width = own.shape[2:]
    reach = k_scr.shape[0] // tokens - 1

    def place(i, block):
        k_scr[i * tokens : (i + 1) * tokens, :] = block[0, 0]
        v_scr[i * tokens : (i + 1) * tokens, :] = block[1, 0]

    place(0, far)
    place(2, near)
    place(4, own)

    @pl.when(low_ref[0] == 1)
    def _():
        place(1, side_far)
        place(3, side_near)

    @pl.when(low_ref[0] == 0)
    def _():
        place(1, side_near)
        place(3, side_own)

    @pl.when(pl.program_id(0) == 0)
    def _():
        ks_scr[...] = jnp.zeros_like(ks_scr)
        kx_scr[...] = jnp.zeros_like(kx_scr)
        qs_scr[...] = jnp.zeros_like(qs_scr)
        qx_scr[...] = jnp.zeros_like(qx_scr)

    kt_scr[...] = k_scr[...].T
    span = bias_ref.shape[1]
    step = span // 3
    lanes = 2 * HALF
    q = q_ref[...].reshape(2 * lanes, width)
    g = g_ref[...].reshape(2 * lanes, width)
    invs, deltas = [], []
    for h in range(2):
        total = jnp.zeros((1, lanes), f32)
        delta = jnp.zeros((1, lanes), f32)
        for j in range(span // step):
            base = h * HALF + j * step
            s = dot(k_scr[base : base + step, :], q[h * lanes : (h + 1) * lanes], NT)
            bias = bias_ref[h, j * step : (j + 1) * step, :]
            e = jnp.exp2(s + jnp.concatenate([bias, bias], 1))
            p = dot(v_scr[base : base + step, :], g[h * lanes : (h + 1) * lanes], NT)
            total = total + jnp.sum(e, axis=0, keepdims=True)
            delta = delta + jnp.sum(e * p, axis=0, keepdims=True)
            e_scr[h, j * step : (j + 1) * step, :] = e
            p_scr[h, j * step : (j + 1) * step, :] = p
        inv = 1.0 / total
        invs.append(inv)
        deltas.append(delta * inv)

    def terms(h, first, rows):
        at = slice(first - h * HALF, first - h * HALF + rows)
        w = e_scr[h, at, :] * invs[h]
        ds = w * (p_scr[h, at, :] - deltas[h])
        return w.astype(bf16), ds.astype(bf16)

    refs = ((even_ref, 0), (odd_ref, 0), (even_ref, 1), (odd_ref, 1))
    dqs = [jnp.zeros((width, lanes), f32) for _ in range(2)]
    pieces = [(0, HALF, (0,))]
    pieces += [(first, HALF, (0, 1)) for first in range(HALF, span, HALF)]
    pieces += [(span, HALF, (1,))]
    for first, rows, halves in pieces:
        found = [terms(h, first, rows) for h in halves]
        w = jnp.concatenate([x[0] for x in found], 1)
        ds = jnp.concatenate([x[1] for x in found], 1)
        used = slice(halves[0] * lanes, (halves[-1] + 1) * lanes)
        dk = dot(ds, q[used])
        dv = dot(w, g[used])
        for h, x in zip(halves, found):
            dqs[h] = dqs[h] + dot(kt_scr[:, first : first + rows], x[1])
        at = slice(first, first + rows)
        k = k_scr[at, :].astype(f32)
        ks_scr[at, :] += dk * k
        kx_scr[at, :] += dk * pltpu.roll(k, 64, 1)
        block, inside = divmod(first, tokens)
        inner = slice(inside, inside + rows)
        dk = dk * math.log(2.0)
        if block < reach:
            ref, which = refs[block]
            ref[which, 0, 0, inner, :] = dk.astype(bf16)
            ref[which, 1, 0, inner, :] = dv.astype(bf16)
        else:
            own_ref[0, 0, inner, :] = dk
            own_ref[1, 0, inner, :] = dv
    for h in range(2):
        dq = (dqs[h] * attn_scale).T
        dq_ref[0, h] = dq.reshape(2, HALF, width)
        x = q[h * lanes : (h + 1) * lanes].astype(f32)
        at = slice(h * lanes, (h + 1) * lanes)
        qs_scr[at, :] += dq * x
        qx_scr[at, :] += dq * pltpu.roll(x, 64, 1)

    @pl.when(pl.program_id(0) == pl.num_programs(0) - 1)
    def _():
        query = jnp.zeros((1, width), f32)
        for h in range(2):
            rows = slice(h * HALF, (h + 1) * HALF)
            for r in range(2):
                at = slice(h * lanes + r * HALF, h * lanes + (r + 1) * HALF)
                query = query + turned_sum(
                    qs_scr[at, :], qx_scr[at, :], cos_ref[rows, :], sin_ref[rows, :]
                )
        key = jnp.zeros((1, width), f32)
        for i in range(reach + 1):
            cb, sb = shift_ref[2 * i : 2 * i + 1, :], shift_ref[2 * i + 1 : 2 * i + 2, :]
            cos = cos_ref[...] * cb + sin_ref[...] * sb
            sin = sin_ref[...] * cb - cos_ref[...] * sb
            at = slice(i * tokens, (i + 1) * tokens)
            key = key + turned_sum(ks_scr[at, :], kx_scr[at, :], cos, sin)
        gain_ref[0:1, :] = query
        gain_ref[1:2, :] = key * math.log(2.0)


def norm_back(dn, x, gain):
    inv = lax.rsqrt(jnp.mean(x * x, axis=-1, keepdims=True) + norm_eps)
    unit = x * inv
    gu = dn * gain
    return inv * (gu - unit * jnp.mean(gu * unit, axis=-1, keepdims=True))


def query_end_kernel(q_ref, gain_ref, cos_ref, sin_ref, *rest):
    dq_refs, out_ref, scr, res = rest[:-3], rest[-3], rest[-2], rest[-1]
    tokens, heads, width = q_ref.shape
    scr[...] = q_ref[...].astype(f32).reshape(tokens * heads, width)
    head = 0
    for dq_ref in dq_refs:
        for i in range(dq_ref.shape[0]):
            for r in range(2):
                rows = pl.ds(head, tokens, stride=heads)
                dn = unturn(dq_ref[i, 0, r], cos_ref[...], sin_ref[...])
                res[rows, :] = norm_back(dn, scr[rows, :], gain_ref[...])
                head += 1
    out_ref[...] = res[...].reshape(tokens, heads, width).astype(bf16)


def key_end_kernel(low_ref, k_ref, gain_ref, cos_ref, sin_ref, *rest):
    kg_ref, vg_ref, scr, res = rest[-4:]
    parts = rest[:-4]
    tokens, heads, width = k_ref.shape
    scr[...] = k_ref[...].astype(f32).reshape(tokens * heads, width)
    low = low_ref[0].astype(f32)
    head = 0
    for c in range(len(parts) // 3):
        own, other, came = parts[3 * c : 3 * c + 3]
        for i in range(own.shape[1]):
            rows = pl.ds(head, tokens, stride=heads)
            dk = own[0, i] + other[0, 0, i].astype(f32) * low + came[0, i].astype(f32)
            dn = unturn(dk, cos_ref[...], sin_ref[...])
            res[0, rows, :] = norm_back(dn, scr[rows, :], gain_ref[...])
            res[1, rows, :] = own[1, i] + other[0, 1, i].astype(f32) * low + came[1, i].astype(f32)
            head += 1
    kg_ref[...] = res[0].reshape(tokens, heads, width).astype(bf16)
    vg_ref[...] = res[1].reshape(tokens, heads, width).astype(bf16)


def call(kernel, grid, in_specs, out_specs, outs, scratch, cost):
    return pl.pallas_call(
        kernel,
        grid=(grid,),
        in_specs=in_specs,
        out_specs=out_specs,
        out_shape=outs,
        scratch_shapes=scratch,
        compiler_params=pltpu.CompilerParams(vmem_limit_bytes=VMEM_LIMIT),
        cost_estimate=pl.CostEstimate(flops=cost[0], bytes_accessed=cost[1], transcendentals=0),
    )


def at_rest(*shape):
    return pl.BlockSpec(shape, lambda i: (0,) * len(shape))


def body(queries, keys, values, output_gradient, window_start, query_gain, key_gain):
    tokens, heads, width = queries.shape
    groups = keys.shape[1]
    reach = WINDOW_LENGTH // tokens
    span = WINDOW_LENGTH + HALF
    full = WINDOW_LENGTH + tokens
    halves = tokens // HALF
    index = lax.axis_index("seq")
    first = index * tokens
    low = lax.rem(index, 2) == 0
    flag = low.astype(jnp.int32)[None]
    cos, sin = rope_tables(first + jnp.arange(tokens, dtype=jnp.int32), width)
    shift = jnp.asarray(shift_table(tokens, reach, width))
    sds = jax.ShapeDtypeStruct
    mib = 1 << 20
    smem = pl.BlockSpec(memory_space=pltpu.SMEM)
    row_spec = pl.BlockSpec((TILE, width), lambda i: (i, 0))
    kv_tile = pl.BlockSpec((TILE, groups, width), lambda i: (i, 0, 0))
    q_tile = pl.BlockSpec((TILE, heads, width), lambda i: (i, 0, 0))
    per_half = HALF // TILE

    def half_spec(count):
        return pl.BlockSpec(
            (count, 1, 2, TILE, width), lambda i: (0, i // per_half, 0, i % per_half, 0)
        )

    def part_spec(count):
        return pl.BlockSpec((2, count, TILE, width), lambda i: (0, 0, i, 0))

    own = call(
        key_prep_kernel,
        tokens // TILE,
        [kv_tile, kv_tile, at_rest(1, width), row_spec, row_spec],
        [part_spec(n) for n in SPLIT],
        [sds((2, n, tokens, width), bf16) for n in SPLIT],
        [pltpu.VMEM((2, TILE * groups, width), f32)],
        (8 * mib, 2 * mib),
    )(keys, values, key_gain[None, :], cos, sin)
    near, far, side_own, side_near, side_far = [], [], [], [], []
    for c in range(len(SPLIT)):
        near.append(hop(own[c], 2))
        far.append(hop(near[c], 2))
        side_own.append(swap(own[c], (0,)))
        side_near.append(swap(near[c]))
        side_far.append(swap(far[c], (1,)))

    starts = (window_start - first + WINDOW_LENGTH).reshape(halves, 1, HALF)
    qs, go, bias = call(
        query_prep_kernel,
        tokens // TILE,
        [
            q_tile,
            q_tile,
            pl.BlockSpec((1, 1, HALF), lambda i: (i // per_half, 0, 0)),
            at_rest(1, width),
            row_spec,
            row_spec,
        ],
        [
            half_spec(groups),
            half_spec(groups),
            pl.BlockSpec((1, span, HALF), lambda i: (i // per_half, 0, 0)),
        ],
        [sds((groups, halves, 2, HALF, width), bf16)] * 2 + [sds((halves, span, HALF), f32)],
        [pltpu.VMEM((2, TILE * heads, width), f32)],
        (16 * mib, 5 * mib),
    )(queries, output_gradient, starts, query_gain[None, :], cos, sin)

    kv_spec = pl.BlockSpec((2, 1, tokens, width), lambda i: (0, i, 0, 0))
    term_spec = pl.BlockSpec((2, 2, 1, tokens, width), lambda i: (0, 0, i, 0, 0))
    unit = (1, halves, 2, HALF, width)
    gains = jnp.zeros((2, width), f32)
    dqs, ends = [], []
    base = 0
    for c, per in enumerate(SPLIT):
        q_spec = pl.BlockSpec(unit, lambda i, base=base: (base + i, 0, 0, 0, 0))
        base += per
        attend = call(
            main_kernel,
            per,
            [smem]
            + [kv_spec] * 6
            + [q_spec] * 2
            + [at_rest(halves, span, HALF)]
            + [at_rest(tokens, width)] * 2
            + [at_rest(2 * (reach + 1), width)],
            [
                term_spec,
                term_spec,
                kv_spec,
                pl.BlockSpec(unit, lambda i: (i, 0, 0, 0, 0)),
                at_rest(2, width),
            ],
            [
                sds((2, 2, per, tokens, width), bf16),
                sds((2, 2, per, tokens, width), bf16),
                sds((2, per, tokens, width), f32),
                sds((per, *unit[1:]), f32),
                sds((2, width), f32),
            ],
            [
                pltpu.VMEM((full, width), bf16),
                pltpu.VMEM((full, width), bf16),
                pltpu.VMEM((width, full), bf16),
                pltpu.VMEM((halves, span, 2 * HALF), f32),
                pltpu.VMEM((halves, span, 2 * HALF), f32),
                pltpu.VMEM((full, width), f32),
                pltpu.VMEM((full, width), f32),
                pltpu.VMEM((2 * tokens, width), f32),
                pltpu.VMEM((2 * tokens, width), f32),
            ],
            (2 * per * 2 * 5 * span * 2 * HALF * width * 2, per * 2 * mib),
        )
        odd, even, mine, dq, gain = attend(
            flag, far[c], near[c], own[c], side_own[c], side_near[c], side_far[c],
            qs, go, bias, cos, sin, shift,
        )
        gains = gains + gain
        dqs.append(dq)
        other = swap(odd)
        send_far = even[0] + jnp.where(low, jnp.zeros_like(other[0]), other[0])
        came_far = hop(send_far, -2)
        send_near = even[1] + jnp.where(low, other[0], other[1]) + came_far
        ends += [mine, other, hop(send_near, -2)]

    factor = jnp.stack([1.0 / (query_gain * query_scale), 1.0 / key_gain])
    gains = all_sum(gains * factor)

    query_grad = call(
        query_end_kernel,
        tokens // TILE,
        [q_tile, at_rest(1, width), row_spec, row_spec] + [half_spec(n) for n in SPLIT],
        q_tile,
        sds((tokens, heads, width), bf16),
        [pltpu.VMEM((TILE * heads, width), f32)] * 2,
        (16 * mib, 4 * mib),
    )(queries, query_gain[None, :], cos, sin, *dqs)
    specs = []
    for n in SPLIT:
        other_spec = pl.BlockSpec((1, 2, n, TILE, width), lambda i: (1, 0, 0, i, 0))
        specs += [part_spec(n), other_spec, part_spec(n)]
    key_grad, value_grad = call(
        key_end_kernel,
        tokens // TILE,
        [smem, kv_tile, at_rest(1, width), row_spec, row_spec] + specs,
        [kv_tile] * 2,
        [sds((tokens, groups, width), bf16)] * 2,
        [
            pltpu.VMEM((TILE * groups, width), f32),
            pltpu.VMEM((2, TILE * groups, width), f32),
        ],
        (8 * mib, 4 * mib),
    )(flag, keys, key_gain[None, :], cos, sin, *ends)
    return query_grad, key_grad, value_grad, gains[0], gains[1]


def solution(mesh):
    wide = P("seq", "kv", None)
    return jax.shard_map(
        body,
        mesh=mesh,
        in_specs=(wide, wide, wide, wide, P("seq"), P(), P()),
        out_specs=(wide, wide, wide, P(), P()),
        check_vma=False,
    )
```

time: 181 us -> 165 us (0.912)
  waiting for transfers between devices: 56.2 us -> 39.5 us
  starting transfers between devices: 47.4 us -> 62.2 us
  other arithmetic: 15.3 us -> 3.6 us
    ppermute x18 -> x20, starting transfers between devices: 19.4 us -> 29.6 us  [the longest x12 18.8 us: all_sum(): lax.ppermute(value, ('seq', 'kv'), list(enumerate(target)))]
    ppermute x18 -> x20, waiting for transfers between devices: 14 us -> 4.71 us  [the longest x12 4.69 us: all_sum(): lax.ppermute(value, ('seq', 'kv'), list(enumerate(target)))]
    ppermute x8, waiting for transfers between devices: 42.1 us -> 34.8 us  [hop(): lax.ppermute(value, 'seq', [(s, s + steps) for s in range(first, last)])]
    ppermute x8, starting transfers between devices: 28 us -> 32.6 us  [hop(): lax.ppermute(value, 'seq', [(s, s + steps) for s in range(first, last)])]
    add x2, other arithmetic: 3.18 us -> 0.12 us  [body(): send_far = even[0] + jnp.where(low, jnp.zeros_like(other[0]), other[0])]
    neg x2 -> x0, other arithmetic: 2.89 us -> none  [rope_tables(): return (jnp.concatenate([cos, cos], -1), jnp.concatenate([-sin, sin], -1))]
    add x2, other arithmetic: 3.08 us -> 0.2 us  [body(): send_near = even[1] + jnp.where(low, other[0], other[1]) + came_far]
    select_n x2 -> x1, other arithmetic: 2.46 us -> 0.01 us  [rope_tables(): sign = jnp.where(jnp.arange(width) < half, -1.0, 1.0).astype(f32)]
  transfers between devices with their start and end apart: 26 -> 28, of which waited for: 8 -> 7; matrix products, arithmetic and copies ran while one was open for 8% -> 1% of each run, Pallas kernels for 17% -> 27%
where the time goes in v1:
time: 165 us
  starting transfers between devices  62.2 us (38%)
  Pallas kernels  55.7 us (34%)
  waiting for transfers between devices  39.5 us (24%)
  other arithmetic  3.6 us (2%)
  local copies, waits for them, and re-layouts  2.3 us (1%)
    ppermute x8, waiting for transfers between devices, hop(): lax.ppermute(value, 'seq', [(s, s + steps) for s in range(first, last)])  34.8 us
    ppermute x8, starting transfers between devices, hop(): lax.ppermute(value, 'seq', [(s, s + steps) for s in range(first, last)])  32.6 us
    pallas_call x2, Pallas kernels, body(): attend(flag, far[c], near[c], own[c], side_own[c], side_near[c], side_far...  26.4 us
    ppermute x12, starting transfers between devices, all_sum(): lax.ppermute(value, ('seq', 'kv'), list(enumerate(target)))  18.8 us
    ppermute x8, starting transfers between devices, swap(): return lax.ppermute(value, 'seq', pairs)  10.8 us
    pallas_call x1, Pallas kernels, body(): call(query_end_kernel, tokens // TILE, [q_tile, at_rest(1, width), row_sp...  9.43 us
    pallas_call x1, Pallas kernels, body(): call(query_prep_kernel, tokens // TILE, [q_tile, q_tile, pl.BlockSpec((1,...  9.31 us
    pallas_call x1, Pallas kernels, body(): call(key_end_kernel, tokens // TILE, [smem, kv_tile, at_rest(1, width), r...  6.05 us
  transfers between devices with their start and end apart: 28, of which 7 were waited for; matrix products, arithmetic and copies ran while one was open for 1% of the time, Pallas kernels for 27%

profile of v1, /device:TPU:24, one launch (start us, length us, event | category | flops | bytes accessed | tf_op | source)
XLA Modules:
  0.0 164.6 jit_solution(15461248055088921652)
XLA Ops:
  0.7 1.2 subtract_add_fusion
  1.9 1.2 fusion.6
  3.1 4.5 %shard_map.119 = (bf16[2,4,256,128]{3,2,1,0:T(8,128)(2,1)}, bf16[2,4,256,128]{3,2,1,0:T(8,128)(2,1)}) custom-call(bf16[256,8,128]{2,1,0:T(8,128)(2,1)} %k_ref.3, bf16[256,8,128]{2,1,0:T(8,128)(2,1)} %v_ref.1, f32[1,128]{1,0:T(1,128)} %bitcast.26, f32[256,128]{1,0:T(8,128)} %get-tuple-element.40.cos_ref, f32[256,128]{1,0:T(8,128)} %get-tuple-element.39.sin_ref), custom_call_target="tpu_custom_call" | custom-call | flops 8388608 | bytes 2097152 | tf_op jit(solution)/shard_map/pallas_call | solution.py:346
  7.7 3.8 %collective-permute-start.5 = (bf16[2,4,256,128]{3,2,1,0:T(8,128)(2,1)}, bf16[2,4,256,128]{3,2,1,0:T(8,128)(2,1)S(1)}, u32[]{:S(2)}, u32[]{:S(2)}) collective-permute-start(bf16[2,4,256,128]{3,2,1,0:T(8,128)(2,1)} %get-tuple-element.27.own), channel_id=1, source_target_pairs={{0,4},{2,6},{4,8},{6,10},{8,12},{10,14},{12,16},{14,18},{16,20},{1... | collective-permute-start | bytes 1572872 | tf_op jit(solution)/shard_map/ppermute | solution.py:29
  11.5 3.8 %collective-permute-start = (bf16[2,4,256,128]{3,2,1,0:T(8,128)(2,1)}, bf16[2,4,256,128]{3,2,1,0:T(8,128)(2,1)S(1)}, u32[]{:S(2)}, u32[]{:S(2)}) collective-permute-start(bf16[2,4,256,128]{3,2,1,0:T(8,128)(2,1)} %get-tuple-element.22.own), channel_id=1, source_target_pairs={{0,4},{2,6},{4,8},{6,10},{8,12},{10,14},{12,16},{14,18},{16,20},{1... | collective-permute-start | bytes 1572872 | tf_op jit(solution)/shard_map/ppermute | solution.py:29
  15.3 15.7 %collective-permute-done.5.near = bf16[2,4,256,128]{3,2,1,0:T(8,128)(2,1)S(1)} collective-permute-done((bf16[2,4,256,128]{3,2,1,0:T(8,128)(2,1)}, bf16[2,4,256,128]{3,2,1,0:T(8,128)(2,1)S(1)}, u32[]{:S(2)}, u32[]{:S(2)}) %collective-permute-start.5) | collective-permute-done | bytes 524320 | tf_op jit(solution)/shard_map/ppermute | solution.py:29
  31.0 1.9 %collective-permute-start.6 = (bf16[2,4,256,128]{3,2,1,0:T(8,128)(2,1)S(1)}, bf16[2,4,256,128]{3,2,1,0:T(8,128)(2,1)S(1)}, u32[]{:S(2)}, u32[]{:S(2)}) collective-permute-start(bf16[2,4,256,128]{3,2,1,0:T(8,128)(2,1)S(1)} %collective-permute-done.5.near), channel_id=1, source_target_pairs={{0,4},{2,6},{4,8},{6,10},{8,12},{10,14},{12,16},{14,18},{16,20},{1... | collective-permute-start | bytes 1572872 | tf_op jit(solution)/shard_map/ppermute | solution.py:29
  32.9 2.1 %collective-permute-start.7 = (bf16[2,4,256,128]{3,2,1,0:T(8,128)(2,1)}, bf16[2,4,256,128]{3,2,1,0:T(8,128)(2,1)}, u32[]{:S(2)}, u32[]{:S(2)}) collective-permute-start(bf16[2,4,256,128]{3,2,1,0:T(8,128)(2,1)} %get-tuple-element.27.own), channel_id=1, source_target_pairs={{0,2},{4,6},{8,10},{12,14},{16,18},{20,22},{24,26},{28,30},{32,34}... | collective-permute-start | bytes 1572872 | tf_op jit(solution)/shard_map/ppermute | solution.py:34
  35.0 7.2 %collective-permute-done.near = bf16[2,4,256,128]{3,2,1,0:T(8,128)(2,1)S(1)} collective-permute-done((bf16[2,4,256,128]{3,2,1,0:T(8,128)(2,1)}, bf16[2,4,256,128]{3,2,1,0:T(8,128)(2,1)S(1)}, u32[]{:S(2)}, u32[]{:S(2)}) %collective-permute-start) | collective-permute-done | bytes 524320 | tf_op jit(solution)/shard_map/ppermute | solution.py:29
  42.3 1.9 %collective-permute-start.1 = (bf16[2,4,256,128]{3,2,1,0:T(8,128)(2,1)S(1)}, bf16[2,4,256,128]{3,2,1,0:T(8,128)(2,1)S(1)}, u32[]{:S(2)}, u32[]{:S(2)}) collective-permute-start(bf16[2,4,256,128]{3,2,1,0:T(8,128)(2,1)S(1)} %collective-permute-done.near), channel_id=1, source_target_pairs={{0,4},{2,6},{4,8},{6,10},{8,12},{10,14},{12,16},{14,18},{16,20},{1... | collective-permute-start | bytes 1572872 | tf_op jit(solution)/shard_map/ppermute | solution.py:29
  44.2 0.1 collective-permute-start.8
  44.3 9.2 %collective-permute-done.6.far = bf16[2,4,256,128]{3,2,1,0:T(8,128)(2,1)S(1)} collective-permute-done((bf16[2,4,256,128]{3,2,1,0:T(8,128)(2,1)S(1)}, bf16[2,4,256,128]{3,2,1,0:T(8,128)(2,1)S(1)}, u32[]{:S(2)}, u32[]{:S(2)}) %collective-permute-start.6) | collective-permute-done | bytes 524320 | tf_op jit(solution)/shard_map/ppermute | solution.py:29
  53.5 1.3 collective-permute-start.9
  54.8 3.8 %collective-permute-start.2 = (bf16[2,4,256,128]{3,2,1,0:T(8,128)(2,1)}, bf16[2,4,256,128]{3,2,1,0:T(8,128)(2,1)S(1)}, u32[]{:S(2)}, u32[]{:S(2)}) collective-permute-start(bf16[2,4,256,128]{3,2,1,0:T(8,128)(2,1)} %get-tuple-element.22.own), channel_id=1, source_target_pairs={{0,2},{4,6},{8,10},{12,14},{16,18},{20,22},{24,26},{28,30},{32,34}... | collective-permute-start | bytes 1572872 | tf_op jit(solution)/shard_map/ppermute | solution.py:34
  58.7 9.3 %shard_map.120 = (bf16[8,2,2,128,128]{4,3,2,1,0:T(8,128)(2,1)}, bf16[8,2,2,128,128]{4,3,2,1,0:T(8,128)(2,1)}, f32[2,1152,128]{2,1,0:T(8,128)}) custom-call(bf16[256,16,128]{2,1,0:T(8,128)(2,1)} %q_ref.3, bf16[256,16,128]{2,1,0:T(8,128)(2,1)} %g_ref.1, s32[2,1,128]{2,1,0:T(1,128)} %bitcast.28, f32[1,128]{1,0:T(1,128)} %bitcast.24, ...), custom_call_target="tpu_custom_call" | custom-call | flops 16777216 | bytes 5242880 | tf_op jit(solution)/shard_map/pallas_call | solution.py:364
  68.0 0.1 collective-permute-start.3
  68.1 1.3 collective-permute-start.4
  69.4 13.2 %shard_map.122 = (bf16[2,2,4,256,128]{4,3,2,1,0:T(8,128)(2,1)}, bf16[2,2,4,256,128]{4,3,2,1,0:T(8,128)(2,1)}, f32[2,4,256,128]{3,2,1,0:T(8,128)}, f32[4,2,2,128,128]{4,3,2,1,0:T(8,128)}, f32[2,128]{1,0:T(2,128)}) custom-call(s32[1]{0:T(128)} %bitcast.1.low_ref, bf16[2,4,256,128]{3,2,1,0:T(8,128)(2,1)} %copy-done.13, bf16[2,4,256,128]{3,2,1,0:T(8,128)(2,1)} %copy-done.11, ...), custom_call_target="tpu_custom_call" | custom-call | flops 6039797760 | bytes 8388608 | tf_op jit(solution)/shard_map/pallas_call | solution.py:430
  82.7 2.0 %collective-permute-start.13 = (bf16[2,2,4,256,128]{4,3,2,1,0:T(8,128)(2,1)}, bf16[2,2,4,256,128]{4,3,2,1,0:T(8,128)(2,1)S(1)}, u32[]{:S(2)}, u32[]{:S(2)}) collective-permute-start(bf16[2,2,4,256,128]{4,3,2,1,0:T(8,128)(2,1)} %get-tuple-element.33), channel_id=1, source_target_pairs={{0,2},{2,0},{4,6},{6,4},{8,10},{10,8},{12,14},{14,12},{16,18},{18,... | collective-permute-start | bytes 3145736 | tf_op jit(solution)/shard_map/ppermute | solution.py:34
  84.7 0.8 copy-done.12
  85.5 13.2 %shard_map.121 = (bf16[2,2,4,256,128]{4,3,2,1,0:T(8,128)(2,1)}, bf16[2,2,4,256,128]{4,3,2,1,0:T(8,128)(2,1)}, f32[2,4,256,128]{3,2,1,0:T(8,128)}, f32[4,2,2,128,128]{4,3,2,1,0:T(8,128)}, f32[2,128]{1,0:T(2,128)}) custom-call(s32[1]{0:T(128)} %bitcast.1.low_ref, bf16[2,4,256,128]{3,2,1,0:T(8,128)(2,1)} %copy-done.10, bf16[2,4,256,128]{3,2,1,0:T(8,128)(2,1)} %copy-done.9, ...), custom_call_target="tpu_custom_call" | custom-call | flops 6039797760 | bytes 8388608 | tf_op jit(solution)/shard_map/pallas_call | solution.py:430
  98.8 0.8 maximum_multiply_fusion
  99.6 0.6 collective-permute-start.16
  100.2 0.1 collective-permute-start.17
  100.3 1.4 collective-permute-start.18
  101.8 3.9 %collective-permute-start.14 = (bf16[2,4,256,128]{3,2,1,0:T(8,128)(2,1)S(1)}, bf16[2,4,256,128]{3,2,1,0:T(8,128)(2,1)S(1)}, u32[]{:S(2)}, u32[]{:S(2)}) collective-permute-start(bf16[2,4,256,128]{3,2,1,0:T(8,128)(2,1)S(1)} %add_bitcast_fusion), channel_id=1, source_target_pairs={{4,0},{6,2},{8,4},{10,6},{12,8},{14,10},{16,12},{18,14},{20,16},{2... | collective-permute-start | bytes 1572872 | tf_op jit(solution)/shard_map/ppermute | solution.py:29
  105.9 2.9 %collective-permute-start.11 = (bf16[2,4,256,128]{3,2,1,0:T(8,128)(2,1)S(1)}, bf16[2,4,256,128]{3,2,1,0:T(8,128)(2,1)S(1)}, u32[]{:S(2)}, u32[]{:S(2)}) collective-permute-start(bf16[2,4,256,128]{3,2,1,0:T(8,128)(2,1)S(1)} %add_bitcast_fusion.1), channel_id=1, source_target_pairs={{4,0},{6,2},{8,4},{10,6},{12,8},{14,10},{16,12},{18,14},{20,16},{2... | collective-permute-start | bytes 1572872 | tf_op jit(solution)/shard_map/ppermute | solution.py:29
  108.8 1.1 collective-permute-start.19
  109.9 1.9 %collective-permute-start.21 = (f32[2,128]{1,0:T(2,128)S(1)}, f32[2,128]{1,0:T(2,128)S(1)}, u32[]{:S(2)}, u32[]{:S(2)}) collective-permute-start(f32[2,128]{1,0:T(2,128)S(1)} %add_add_fusion.3), channel_id=1, source_target_pairs={{0,12},{1,13},{2,14},{3,15},{4,16},{5,17},{6,18},{7,19},{8,20},{9,... | collective-permute-start | bytes 3080 | tf_op jit(solution)/shard_map/ppermute | solution.py:53
  111.9 1.8 %collective-permute-done.19 = f32[2,128]{1,0:T(2,128)S(1)} collective-permute-done((f32[2,128]{1,0:T(2,128)S(1)}, f32[2,128]{1,0:T(2,128)S(1)}, u32[]{:S(2)}, u32[]{:S(2)}) %collective-permute-start.19) | collective-permute-done | bytes 1056 | tf_op jit(solution)/shard_map/ppermute | solution.py:53
  113.7 1.9 %collective-permute-done.20 = f32[2,128]{1,0:T(2,128)S(1)} collective-permute-done((f32[2,128]{1,0:T(2,128)S(1)}, f32[2,128]{1,0:T(2,128)S(1)}, u32[]{:S(2)}, u32[]{:S(2)}) %collective-permute-start.20) | collective-permute-done | bytes 1056 | tf_op jit(solution)/shard_map/ppermute | solution.py:53
  115.6 0.9 collective-permute-done.21
  116.5 0.4 collective-permute-start.22
  117.0 0.6 collective-permute-start.23
  117.6 3.7 %collective-permute-start.24 = (f32[2,128]{1,0:T(2,128)S(1)}, f32[2,128]{1,0:T(2,128)S(1)}, u32[]{:S(2)}, u32[]{:S(2)}) collective-permute-start(f32[2,128]{1,0:T(2,128)S(1)} %add_add_fusion.2), channel_id=1, source_target_pairs={{0,192},{1,193},{2,194},{3,195},{4,196},{5,197},{6,198},{7,199},{8... | collective-permute-start | bytes 3080 | tf_op jit(solution)/shard_map/ppermute | solution.py:53
  121.2 0.1 fusion.2
  121.3 5.8 %collective-permute-start.15 = (bf16[2,4,256,128]{3,2,1,0:T(8,128)(2,1)S(1)}, bf16[2,4,256,128]{3,2,1,0:T(8,128)(2,1)S(1)}, u32[]{:S(2)}, u32[]{:S(2)}) collective-permute-start(bf16[2,4,256,128]{3,2,1,0:T(8,128)(2,1)S(1)} %fusion.2), channel_id=1, source_target_pairs={{4,0},{6,2},{8,4},{10,6},{12,8},{14,10},{16,12},{18,14},{20,16},{2... | collective-permute-start | bytes 1572872 | tf_op jit(solution)/shard_map/ppermute | solution.py:29
  127.1 2.6 %collective-permute-done.11 = bf16[2,4,256,128]{3,2,1,0:T(8,128)(2,1)S(1)} collective-permute-done((bf16[2,4,256,128]{3,2,1,0:T(8,128)(2,1)S(1)}, bf16[2,4,256,128]{3,2,1,0:T(8,128)(2,1)S(1)}, u32[]{:S(2)}, u32[]{:S(2)}) %collective-permute-start.11) | collective-permute-done | bytes 524320 | tf_op jit(solution)/shard_map/ppermute | solution.py:29
  129.8 0.1 fusion.5
  129.9 8.5 %collective-permute-start.12 = (bf16[2,4,256,128]{3,2,1,0:T(8,128)(2,1)S(1)}, bf16[2,4,256,128]{3,2,1,0:T(8,128)(2,1)S(1)}, u32[]{:S(2)}, u32[]{:S(2)}) collective-permute-start(bf16[2,4,256,128]{3,2,1,0:T(8,128)(2,1)S(1)} %fusion.5), channel_id=1, source_target_pairs={{4,0},{6,2},{8,4},{10,6},{12,8},{14,10},{16,12},{18,14},{20,16},{2... | collective-permute-start | bytes 1572872 | tf_op jit(solution)/shard_map/ppermute | solution.py:29
  138.4 0.1 collective-permute-start.25
  138.5 0.1 collective-permute-start.26
  138.6 8.8 %collective-permute-start.27 = (f32[2,128]{1,0:T(2,128)S(1)}, f32[2,128]{1,0:T(2,128)S(1)}, u32[]{:S(2)}, u32[]{:S(2)}) collective-permute-start(f32[2,128]{1,0:T(2,128)S(1)} %add_add_fusion.1), channel_id=1, source_target_pairs={{0,48},{1,49},{2,50},{3,51},{4,52},{5,53},{6,54},{7,55},{8,56},{9,... | collective-permute-start | bytes 3080 | tf_op jit(solution)/shard_map/ppermute | solution.py:53
  147.4 9.4 %shard_map.123 = bf16[256,16,128]{2,1,0:T(8,128)(2,1)} custom-call(bf16[256,16,128]{2,1,0:T(8,128)(2,1)} %q_ref.3, f32[1,128]{1,0:T(1,128)} %bitcast.25, f32[256,128]{1,0:T(8,128)} %get-tuple-element.40.cos_ref, f32[256,128]{1,0:T(8,128)} %get-tuple-element.39.sin_ref, f32[4,2,2,128,128]{4,3,2,1,0:T(8,128)} %get-tuple-element.26.rest_0_, ...), custom_call_target="tpu_custom_call" | custom-call | flops 16777216 | bytes 4194304 | tf_op jit(solution)/shard_map/pallas_call | solution.py:445
  156.9 0.5 slice_bitcast_fusion
  157.4 0.8 copy-done.4
  158.2 0.2 copy-done.5
  158.4 6.1 %shard_map.124 = (bf16[256,8,128]{2,1,0:T(8,128)(2,1)}, bf16[256,8,128]{2,1,0:T(8,128)(2,1)}) custom-call(s32[1]{0:T(128)} %bitcast.1.low_ref, bf16[256,8,128]{2,1,0:T(8,128)(2,1)} %k_ref.3, f32[1,128]{1,0:T(1,128)} %bitcast.27, f32[256,128]{1,0:T(8,128)} %get-tuple-element.40.cos_ref, f32[256,128]{1,0:T(8,128)} %get-tuple-element.39.sin_ref, ...), custom_call_target="tpu_custom_call" | custom-call | flops 8388608 | bytes 4194304 | tf_op jit(solution)/shard_map/pallas_call | solution.py:458
  (56 shorter events, 0.4 us)
Async XLA Ops:
  7.7 23.4 %collective-permute-start.5 = (bf16[2,4,256,128]{3,2,1,0:T(8,128)(2,1)}, bf16[2,4,256,128]{3,2,1,0:T(8,128)(2,1)S(1)}, u32[]{:S(2)}, u32[]{:S(2)}) collective-permute-start(bf16[2,4,256,128]{3,2,1,0:T(8,128)(2,1)} %get-tuple-element.27.own), channel_id=1, source_target_pairs={{0,4},{2,6},{4,8},{6,10},{8,12},{10,14},{12,16},{14,18},{16,20},{1... | collective-permute-start | bytes 1572872 | tf_op jit(solution)/shard_map/ppermute | solution.py:29
  11.5 30.8 %collective-permute-start = (bf16[2,4,256,128]{3,2,1,0:T(8,128)(2,1)}, bf16[2,4,256,128]{3,2,1,0:T(8,128)(2,1)S(1)}, u32[]{:S(2)}, u32[]{:S(2)}) collective-permute-start(bf16[2,4,256,128]{3,2,1,0:T(8,128)(2,1)} %get-tuple-element.22.own), channel_id=1, source_target_pairs={{0,4},{2,6},{4,8},{6,10},{8,12},{10,14},{12,16},{14,18},{16,20},{1... | collective-permute-start | bytes 1572872 | tf_op jit(solution)/shard_map/ppermute | solution.py:29
  31.0 36.9 %copy-start.11 = (bf16[2,4,256,128]{3,2,1,0:T(8,128)(2,1)}, bf16[2,4,256,128]{3,2,1,0:T(8,128)(2,1)S(1)}, u32[]{:S(2)}) copy-start(bf16[2,4,256,128]{3,2,1,0:T(8,128)(2,1)S(1)} %collective-permute-done.5.near) | copy-start | bytes 1572868
  31.0 22.5 %collective-permute-start.6 = (bf16[2,4,256,128]{3,2,1,0:T(8,128)(2,1)S(1)}, bf16[2,4,256,128]{3,2,1,0:T(8,128)(2,1)S(1)}, u32[]{:S(2)}, u32[]{:S(2)}) collective-permute-start(bf16[2,4,256,128]{3,2,1,0:T(8,128)(2,1)S(1)} %collective-permute-done.5.near), channel_id=1, source_target_pairs={{0,4},{2,6},{4,8},{6,10},{8,12},{10,14},{12,16},{14,18},{16,20},{1... | collective-permute-start | bytes 1572872 | tf_op jit(solution)/shard_map/ppermute | solution.py:29
  32.9 35.0 %collective-permute-start.7 = (bf16[2,4,256,128]{3,2,1,0:T(8,128)(2,1)}, bf16[2,4,256,128]{3,2,1,0:T(8,128)(2,1)}, u32[]{:S(2)}, u32[]{:S(2)}) collective-permute-start(bf16[2,4,256,128]{3,2,1,0:T(8,128)(2,1)} %get-tuple-element.27.own), channel_id=1, source_target_pairs={{0,2},{4,6},{8,10},{12,14},{16,18},{20,22},{24,26},{28,30},{32,34}... | collective-permute-start | bytes 1572872 | tf_op jit(solution)/shard_map/ppermute | solution.py:34
  42.3 25.7 %copy-start.9 = (bf16[2,4,256,128]{3,2,1,0:T(8,128)(2,1)}, bf16[2,4,256,128]{3,2,1,0:T(8,128)(2,1)S(1)}, u32[]{:S(2)}) copy-start(bf16[2,4,256,128]{3,2,1,0:T(8,128)(2,1)S(1)} %collective-permute-done.near) | copy-start | bytes 1572868
  42.3 25.8 %collective-permute-start.1 = (bf16[2,4,256,128]{3,2,1,0:T(8,128)(2,1)S(1)}, bf16[2,4,256,128]{3,2,1,0:T(8,128)(2,1)S(1)}, u32[]{:S(2)}, u32[]{:S(2)}) collective-permute-start(bf16[2,4,256,128]{3,2,1,0:T(8,128)(2,1)S(1)} %collective-permute-done.near), channel_id=1, source_target_pairs={{0,4},{2,6},{4,8},{6,10},{8,12},{10,14},{12,16},{14,18},{16,20},{1... | collective-permute-start | bytes 1572872 | tf_op jit(solution)/shard_map/ppermute | solution.py:29
  44.2 25.2 %collective-permute-start.8 = (bf16[2,4,256,128]{3,2,1,0:T(8,128)(2,1)S(1)}, bf16[2,4,256,128]{3,2,1,0:T(8,128)(2,1)}, u32[]{:S(2)}, u32[]{:S(2)}) collective-permute-start(bf16[2,4,256,128]{3,2,1,0:T(8,128)(2,1)S(1)} %collective-permute-done.5.near), channel_id=1, source_target_pairs={{0,2},{2,0},{4,6},{6,4},{8,10},{10,8},{12,14},{14,12},{16,18},{18,... | collective-permute-start | bytes 1572872 | tf_op jit(solution)/shard_map/ppermute | solution.py:34
  53.5 14.5 %copy-start.13 = (bf16[2,4,256,128]{3,2,1,0:T(8,128)(2,1)}, bf16[2,4,256,128]{3,2,1,0:T(8,128)(2,1)S(1)}, u32[]{:S(2)}) copy-start(bf16[2,4,256,128]{3,2,1,0:T(8,128)(2,1)S(1)} %collective-permute-done.6.far) | copy-start | bytes 1572868
  53.5 15.9 %collective-permute-start.9 = (bf16[2,4,256,128]{3,2,1,0:T(8,128)(2,1)S(1)}, bf16[2,4,256,128]{3,2,1,0:T(8,128)(2,1)}, u32[]{:S(2)}, u32[]{:S(2)}) collective-permute-start(bf16[2,4,256,128]{3,2,1,0:T(8,128)(2,1)S(1)} %collective-permute-done.6.far), channel_id=1, source_target_pairs={{2,0},{6,4},{10,8},{14,12},{18,16},{22,20},{26,24},{30,28},{34,32}... | collective-permute-start | bytes 1572872 | tf_op jit(solution)/shard_map/ppermute | solution.py:34
  54.8 29.9 %collective-permute-start.2 = (bf16[2,4,256,128]{3,2,1,0:T(8,128)(2,1)}, bf16[2,4,256,128]{3,2,1,0:T(8,128)(2,1)S(1)}, u32[]{:S(2)}, u32[]{:S(2)}) collective-permute-start(bf16[2,4,256,128]{3,2,1,0:T(8,128)(2,1)} %get-tuple-element.22.own), channel_id=1, source_target_pairs={{0,2},{4,6},{8,10},{12,14},{16,18},{20,22},{24,26},{28,30},{32,34}... | collective-permute-start | bytes 1572872 | tf_op jit(solution)/shard_map/ppermute | solution.py:34
  68.0 16.7 %collective-permute-start.3 = (bf16[2,4,256,128]{3,2,1,0:T(8,128)(2,1)S(1)}, bf16[2,4,256,128]{3,2,1,0:T(8,128)(2,1)}, u32[]{:S(2)}, u32[]{:S(2)}) collective-permute-start(bf16[2,4,256,128]{3,2,1,0:T(8,128)(2,1)S(1)} %collective-permute-done.near), channel_id=1, source_target_pairs={{0,2},{2,0},{4,6},{6,4},{8,10},{10,8},{12,14},{14,12},{16,18},{18,... | collective-permute-start | bytes 1572872 | tf_op jit(solution)/shard_map/ppermute | solution.py:34
  68.1 14.6 %copy-start.10 = (bf16[2,4,256,128]{3,2,1,0:T(8,128)(2,1)}, bf16[2,4,256,128]{3,2,1,0:T(8,128)(2,1)S(1)}, u32[]{:S(2)}) copy-start(bf16[2,4,256,128]{3,2,1,0:T(8,128)(2,1)S(1)} %collective-permute-done.1.far) | copy-start | bytes 1572868
  68.1 16.6 %collective-permute-start.4 = (bf16[2,4,256,128]{3,2,1,0:T(8,128)(2,1)S(1)}, bf16[2,4,256,128]{3,2,1,0:T(8,128)(2,1)}, u32[]{:S(2)}, u32[]{:S(2)}) collective-permute-start(bf16[2,4,256,128]{3,2,1,0:T(8,128)(2,1)S(1)} %collective-permute-done.1.far), channel_id=1, source_target_pairs={{2,0},{6,4},{10,8},{14,12},{18,16},{22,20},{26,24},{30,28},{34,32}... | collective-permute-start | bytes 1572872 | tf_op jit(solution)/shard_map/ppermute | solution.py:34
  82.7 16.1 %copy-start.6 = (f32[128]{0:T(128)S(1)}, f32[128]{0:T(128)}, u32[]{:S(2)}) copy-start(f32[128]{0:T(128)} %param.13) | copy-start | bytes 1540
  82.7 16.1 %copy-start.7 = (f32[128]{0:T(128)S(1)}, f32[128]{0:T(128)}, u32[]{:S(2)}) copy-start(f32[128]{0:T(128)} %param.14) | copy-start | bytes 1540
  82.7 16.1 %copy-start.8 = (f32[2,128]{1,0:T(2,128)S(1)}, f32[2,128]{1,0:T(2,128)}, u32[]{:S(2)}) copy-start(f32[2,128]{1,0:T(2,128)} %get-tuple-element.38) | copy-start | bytes 3076
  82.7 19.1 %copy-start.2 = (bf16[2,2,4,256,128]{4,3,2,1,0:T(8,128)(2,1)S(1)}, bf16[2,2,4,256,128]{4,3,2,1,0:T(8,128)(2,1)}, u32[]{:S(2)}) copy-start(bf16[2,2,4,256,128]{4,3,2,1,0:T(8,128)(2,1)} %get-tuple-element.34) | copy-start | bytes 3145732
  82.7 19.1 %collective-permute-start.13 = (bf16[2,2,4,256,128]{4,3,2,1,0:T(8,128)(2,1)}, bf16[2,2,4,256,128]{4,3,2,1,0:T(8,128)(2,1)S(1)}, u32[]{:S(2)}, u32[]{:S(2)}) collective-permute-start(bf16[2,2,4,256,128]{4,3,2,1,0:T(8,128)(2,1)} %get-tuple-element.33), channel_id=1, source_target_pairs={{0,2},{2,0},{4,6},{6,4},{8,10},{10,8},{12,14},{14,12},{16,18},{18,... | collective-permute-start | bytes 3145736 | tf_op jit(solution)/shard_map/ppermute | solution.py:34
  84.7 0.8 copy-start.12
  98.7 7.1 %copy-start.3 = (bf16[2,2,4,256,128]{4,3,2,1,0:T(8,128)(2,1)S(1)}, bf16[2,2,4,256,128]{4,3,2,1,0:T(8,128)(2,1)}, u32[]{:S(2)}) copy-start(bf16[2,2,4,256,128]{4,3,2,1,0:T(8,128)(2,1)} %get-tuple-element.31) | copy-start | bytes 3145732
  98.7 7.1 %collective-permute-start.10 = (bf16[2,2,4,256,128]{4,3,2,1,0:T(8,128)(2,1)}, bf16[2,2,4,256,128]{4,3,2,1,0:T(8,128)(2,1)S(1)}, u32[]{:S(2)}, u32[]{:S(2)}) collective-permute-start(bf16[2,2,4,256,128]{4,3,2,1,0:T(8,128)(2,1)} %get-tuple-element.30), channel_id=1, source_target_pairs={{0,2},{2,0},{4,6},{6,4},{8,10},{10,8},{12,14},{14,12},{16,18},{18,... | collective-permute-start | bytes 3145736 | tf_op jit(solution)/shard_map/ppermute | solution.py:34
  99.6 9.2 %collective-permute-start.16 = (f32[2,128]{1,0:T(2,128)S(1)}, f32[2,128]{1,0:T(2,128)S(1)}, u32[]{:S(2)}, u32[]{:S(2)}) collective-permute-start(f32[2,128]{1,0:T(2,128)S(1)} %maximum_multiply_fusion), channel_id=1, source_target_pairs={{0,1},{1,0},{2,3},{3,2},{4,5},{5,4},{6,7},{7,6},{8,9},{9,8},{10,11... | collective-permute-start | bytes 3080 | tf_op jit(solution)/shard_map/ppermute | solution.py:53
  100.2 8.6 %collective-permute-start.17 = (f32[2,128]{1,0:T(2,128)S(1)}, f32[2,128]{1,0:T(2,128)S(1)}, u32[]{:S(2)}, u32[]{:S(2)}) collective-permute-start(f32[2,128]{1,0:T(2,128)S(1)} %maximum_multiply_fusion), channel_id=1, source_target_pairs={{0,2},{1,3},{2,0},{3,1},{4,6},{5,7},{6,4},{7,5},{8,10},{9,11},{10,... | collective-permute-start | bytes 3080 | tf_op jit(solution)/shard_map/ppermute | solution.py:53
  100.3 8.5 %collective-permute-start.18 = (f32[2,128]{1,0:T(2,128)S(1)}, f32[2,128]{1,0:T(2,128)S(1)}, u32[]{:S(2)}, u32[]{:S(2)}) collective-permute-start(f32[2,128]{1,0:T(2,128)S(1)} %maximum_multiply_fusion), channel_id=1, source_target_pairs={{0,3},{1,2},{2,1},{3,0},{4,7},{5,6},{6,5},{7,4},{8,11},{9,10},{10,... | collective-permute-start | bytes 3080 | tf_op jit(solution)/shard_map/ppermute | solution.py:53
  101.8 19.5 %copy-start = (bf16[2,2,4,256,128]{4,3,2,1,0:T(8,128)(2,1)}, bf16[2,2,4,256,128]{4,3,2,1,0:T(8,128)(2,1)S(1)}, u32[]{:S(2)}) copy-start(bf16[2,2,4,256,128]{4,3,2,1,0:T(8,128)(2,1)S(1)} %collective-permute-done.13.rest_4_) | copy-start | bytes 3145732
  101.8 19.4 %collective-permute-start.14 = (bf16[2,4,256,128]{3,2,1,0:T(8,128)(2,1)S(1)}, bf16[2,4,256,128]{3,2,1,0:T(8,128)(2,1)S(1)}, u32[]{:S(2)}, u32[]{:S(2)}) collective-permute-start(bf16[2,4,256,128]{3,2,1,0:T(8,128)(2,1)S(1)} %add_bitcast_fusion), channel_id=1, source_target_pairs={{4,0},{6,2},{8,4},{10,6},{12,8},{14,10},{16,12},{18,14},{20,16},{2... | collective-permute-start | bytes 1572872 | tf_op jit(solution)/shard_map/ppermute | solution.py:29
  105.8 24.0 %copy-start.1 = (bf16[2,2,4,256,128]{4,3,2,1,0:T(8,128)(2,1)}, bf16[2,2,4,256,128]{4,3,2,1,0:T(8,128)(2,1)S(1)}, u32[]{:S(2)}) copy-start(bf16[2,2,4,256,128]{4,3,2,1,0:T(8,128)(2,1)S(1)} %collective-permute-done.10.rest_1_) | copy-start | bytes 3145732
  105.9 23.9 %collective-permute-start.11 = (bf16[2,4,256,128]{3,2,1,0:T(8,128)(2,1)S(1)}, bf16[2,4,256,128]{3,2,1,0:T(8,128)(2,1)S(1)}, u32[]{:S(2)}, u32[]{:S(2)}) collective-permute-start(bf16[2,4,256,128]{3,2,1,0:T(8,128)(2,1)S(1)} %add_bitcast_fusion.1), channel_id=1, source_target_pairs={{4,0},{6,2},{8,4},{10,6},{12,8},{14,10},{16,12},{18,14},{20,16},{2... | collective-permute-start | bytes 1572872 | tf_op jit(solution)/shard_map/ppermute | solution.py:29
  108.8 4.9 %collective-permute-start.19 = (f32[2,128]{1,0:T(2,128)S(1)}, f32[2,128]{1,0:T(2,128)S(1)}, u32[]{:S(2)}, u32[]{:S(2)}) collective-permute-start(f32[2,128]{1,0:T(2,128)S(1)} %add_add_fusion.3), channel_id=1, source_target_pairs={{0,4},{1,5},{2,6},{3,7},{4,8},{5,9},{6,10},{7,11},{8,12},{9,13},{1... | collective-permute-start | bytes 3080 | tf_op jit(solution)/shard_map/ppermute | solution.py:53
  109.9 5.7 %collective-permute-start.20 = (f32[2,128]{1,0:T(2,128)S(1)}, f32[2,128]{1,0:T(2,128)S(1)}, u32[]{:S(2)}, u32[]{:S(2)}) collective-permute-start(f32[2,128]{1,0:T(2,128)S(1)} %add_add_fusion.3), channel_id=1, source_target_pairs={{0,8},{1,9},{2,10},{3,11},{4,12},{5,13},{6,14},{7,15},{8,16},{9,17... | collective-permute-start | bytes 3080 | tf_op jit(solution)/shard_map/ppermute | solution.py:53
  109.9 6.6 %collective-permute-start.21 = (f32[2,128]{1,0:T(2,128)S(1)}, f32[2,128]{1,0:T(2,128)S(1)}, u32[]{:S(2)}, u32[]{:S(2)}) collective-permute-start(f32[2,128]{1,0:T(2,128)S(1)} %add_add_fusion.3), channel_id=1, source_target_pairs={{0,12},{1,13},{2,14},{3,15},{4,16},{5,17},{6,18},{7,19},{8,20},{9,... | collective-permute-start | bytes 3080 | tf_op jit(solution)/shard_map/ppermute | solution.py:53
  116.5 21.8 %collective-permute-start.22 = (f32[2,128]{1,0:T(2,128)S(1)}, f32[2,128]{1,0:T(2,128)S(1)}, u32[]{:S(2)}, u32[]{:S(2)}) collective-permute-start(f32[2,128]{1,0:T(2,128)S(1)} %add_add_fusion.2), channel_id=1, source_target_pairs={{0,64},{1,65},{2,66},{3,67},{4,68},{5,69},{6,70},{7,71},{8,72},{9,... | collective-permute-start | bytes 3080 | tf_op jit(solution)/shard_map/ppermute | solution.py:53
  117.0 21.4 %collective-permute-start.23 = (f32[2,128]{1,0:T(2,128)S(1)}, f32[2,128]{1,0:T(2,128)S(1)}, u32[]{:S(2)}, u32[]{:S(2)}) collective-permute-start(f32[2,128]{1,0:T(2,128)S(1)} %add_add_fusion.2), channel_id=1, source_target_pairs={{0,128},{1,129},{2,130},{3,131},{4,132},{5,133},{6,134},{7,135},{8... | collective-permute-start | bytes 3080 | tf_op jit(solution)/shard_map/ppermute | solution.py:53
  117.6 20.8 %collective-permute-start.24 = (f32[2,128]{1,0:T(2,128)S(1)}, f32[2,128]{1,0:T(2,128)S(1)}, u32[]{:S(2)}, u32[]{:S(2)}) collective-permute-start(f32[2,128]{1,0:T(2,128)S(1)} %add_add_fusion.2), channel_id=1, source_target_pairs={{0,192},{1,193},{2,194},{3,195},{4,196},{5,197},{6,198},{7,199},{8... | collective-permute-start | bytes 3080 | tf_op jit(solution)/shard_map/ppermute | solution.py:53
  121.3 36.0 %collective-permute-start.15 = (bf16[2,4,256,128]{3,2,1,0:T(8,128)(2,1)S(1)}, bf16[2,4,256,128]{3,2,1,0:T(8,128)(2,1)S(1)}, u32[]{:S(2)}, u32[]{:S(2)}) collective-permute-start(bf16[2,4,256,128]{3,2,1,0:T(8,128)(2,1)S(1)} %fusion.2), channel_id=1, source_target_pairs={{4,0},{6,2},{8,4},{10,6},{12,8},{14,10},{16,12},{18,14},{20,16},{2... | collective-permute-start | bytes 1572872 | tf_op jit(solution)/shard_map/ppermute | solution.py:29
  129.9 27.5 %collective-permute-start.12 = (bf16[2,4,256,128]{3,2,1,0:T(8,128)(2,1)S(1)}, bf16[2,4,256,128]{3,2,1,0:T(8,128)(2,1)S(1)}, u32[]{:S(2)}, u32[]{:S(2)}) collective-permute-start(bf16[2,4,256,128]{3,2,1,0:T(8,128)(2,1)S(1)} %fusion.5), channel_id=1, source_target_pairs={{4,0},{6,2},{8,4},{10,6},{12,8},{14,10},{16,12},{18,14},{20,16},{2... | collective-permute-start | bytes 1572872 | tf_op jit(solution)/shard_map/ppermute | solution.py:29
  138.4 18.4 %collective-permute-start.25 = (f32[2,128]{1,0:T(2,128)S(1)}, f32[2,128]{1,0:T(2,128)S(1)}, u32[]{:S(2)}, u32[]{:S(2)}) collective-permute-start(f32[2,128]{1,0:T(2,128)S(1)} %add_add_fusion.1), channel_id=1, source_target_pairs={{0,16},{1,17},{2,18},{3,19},{4,20},{5,21},{6,22},{7,23},{8,24},{9,... | collective-permute-start | bytes 3080 | tf_op jit(solution)/shard_map/ppermute | solution.py:53
  138.5 18.3 %collective-permute-start.26 = (f32[2,128]{1,0:T(2,128)S(1)}, f32[2,128]{1,0:T(2,128)S(1)}, u32[]{:S(2)}, u32[]{:S(2)}) collective-permute-start(f32[2,128]{1,0:T(2,128)S(1)} %add_add_fusion.1), channel_id=1, source_target_pairs={{0,32},{1,33},{2,34},{3,35},{4,36},{5,37},{6,38},{7,39},{8,40},{9,... | collective-permute-start | bytes 3080 | tf_op jit(solution)/shard_map/ppermute | solution.py:53
  138.6 18.2 %collective-permute-start.27 = (f32[2,128]{1,0:T(2,128)S(1)}, f32[2,128]{1,0:T(2,128)S(1)}, u32[]{:S(2)}, u32[]{:S(2)}) collective-permute-start(f32[2,128]{1,0:T(2,128)S(1)} %add_add_fusion.1), channel_id=1, source_target_pairs={{0,48},{1,49},{2,50},{3,51},{4,52},{5,53},{6,54},{7,55},{8,56},{9,... | collective-permute-start | bytes 3080 | tf_op jit(solution)/shard_map/ppermute | solution.py:53
  157.4 0.8 copy-start.4
  157.4 1.0 copy-start.5

commit v2 on v1

--- a/solution.py
+++ b/solution.py
@@ -29,9 +29,8 @@
     return lax.ppermute(value, "seq", [(s, s + steps) for s in range(first, last)])
 
 
-def swap(value, cores=(0, 1)):
-    pairs = [(s, s ^ 1) for s in range(lax.axis_size("seq")) if s % 2 in cores]
-    return lax.ppermute(value, "seq", pairs)
+def swap(value):
+    return lax.ppermute(value, "seq", [(s, s ^ 1) for s in range(lax.axis_size("seq"))])
 
 
 def sum_rounds(count):
@@ -80,33 +79,57 @@
     return x * cos - pltpu.roll(x, 64, 1) * sin
 
 
+NT = (((1,), (1,)), ((), ()))
+
+
+def dot(a, b, dims=(((1,), (0,)), ((), ()))):
+    return lax.dot_general(a, b, dims, preferred_element_type=f32)
+
+
+def row_mean(x):
+    high = x.astype(bf16)
+    rest = (x - high.astype(f32)).astype(bf16)
+    share = jnp.full((x.shape[1], x.shape[1]), 1.0 / x.shape[1], bf16)
+    return dot(high, share) + dot(rest, share)
+
+
+def flat(ref):
+    tokens, heads, width = ref.shape
+    return ref[...].astype(f32).reshape(tokens * heads, width)
+
+
+def inverse(x):
+    return lax.rsqrt(row_mean(x * x) + norm_eps)
+
+
 def key_prep_kernel(k_ref, v_ref, gain_ref, cos_ref, sin_ref, *rest):
     out_refs, scr = rest[:-1], rest[-1]
-    tokens, heads, width = k_ref.shape
-    scr[0] = k_ref[...].astype(f32).reshape(tokens * heads, width)
-    scr[1] = v_ref[...].astype(f32).reshape(tokens * heads, width)
+    tokens, heads, _ = k_ref.shape
+    x = flat(k_ref)
+    scr[0] = x * inverse(x) * gain_ref[...]
+    scr[1] = flat(v_ref)
+    cos, sin = cos_ref[...], sin_ref[...]
     head = 0
     for out in out_refs:
         for i in range(out.shape[1]):
-            x = scr[0, pl.ds(head, tokens, stride=heads), :]
-            inv = lax.rsqrt(jnp.mean(x * x, axis=-1, keepdims=True) + norm_eps)
-            x = x * inv * gain_ref[...]
-            out[0, i] = turn(x, cos_ref[...], sin_ref[...]).astype(bf16)
-            out[1, i] = scr[1, pl.ds(head, tokens, stride=heads), :].astype(bf16)
+            rows = pl.ds(head, tokens, stride=heads)
+            out[0, i] = turn(scr[0, rows, :], cos, sin).astype(bf16)
+            out[1, i] = scr[1, rows, :].astype(bf16)
             head += 1
 
 
-def query_prep_kernel(q_ref, g_ref, start_ref, gain_ref, cos_ref, sin_ref, qs_ref, go_ref, bias_ref, scr):
-    tokens, heads, width = q_ref.shape
-    scr[0] = q_ref[...].astype(f32).reshape(tokens * heads, width)
-    scr[1] = g_ref[...].astype(f32).reshape(tokens * heads, width)
+def query_prep_kernel(
+    first_ref, q_ref, g_ref, start_ref, gain_ref, cos_ref, sin_ref, qs_ref, go_ref, bias_ref, scr
+):
+    tokens, heads, _ = q_ref.shape
+    x = flat(q_ref)
+    scr[0] = x * inverse(x) * (gain_ref[...] * query_scale)
+    scr[1] = flat(g_ref)
+    cos, sin = cos_ref[...], sin_ref[...]
     for group in range(heads // 2):
         for r in range(2):
             rows = pl.ds(2 * group + r, tokens, stride=heads)
-            x = scr[0, rows, :]
-            inv = lax.rsqrt(jnp.mean(x * x, axis=-1, keepdims=True) + norm_eps) * query_scale
-            x = x * inv * gain_ref[...]
-            qs_ref[group, 0, r] = turn(x, cos_ref[...], sin_ref[...]).astype(bf16)
+            qs_ref[group, 0, r] = turn(scr[0, rows, :], cos, sin).astype(bf16)
             go_ref[group, 0, r] = scr[1, rows, :].astype(bf16)
     step = pl.program_id(0)
     per = HALF // tokens
@@ -117,15 +140,9 @@
         shape = bias_ref.shape[1:]
         key = lax.broadcasted_iota(jnp.int32, shape, 0) + offset
         token = lax.broadcasted_iota(jnp.int32, shape, 1) + offset
-        seen = (key >= start_ref[0]) & (key <= token + WINDOW_LENGTH)
+        start = start_ref[0] - first_ref[0] + WINDOW_LENGTH
+        seen = (key >= start) & (key <= token + WINDOW_LENGTH)
         bias_ref[0] = jnp.where(seen, 0.0, -1e30).astype(f32)
-
-
-NT = (((1,), (1,)), ((), ()))
-
-
-def dot(a, b, dims=(((1,), (0,)), ((), ()))):
-    return lax.dot_general(a, b, dims, preferred_element_type=f32)
 
 
 def turned_sum(same, cross, cos, sin):
@@ -138,7 +155,7 @@
 def main_kernel(
     low_ref, far, near, own, side_own, side_near, side_far, q_ref, g_ref, bias_ref, cos_ref, sin_ref, shift_ref,
     odd_ref, even_ref, own_ref, dq_ref, gain_ref,
-    k_scr, v_scr, kt_scr, e_scr, p_scr, ks_scr, kx_scr, qs_scr, qx_scr,
+    k_scr, v_scr, kt_scr, e_scr, p_scr, ds_scr, ks_scr, kx_scr, qs_scr, qx_scr,
 ):
     tokens, width = own.shape[2:]
     reach = k_scr.shape[0] // tokens - 1
@@ -199,7 +216,6 @@
         return w.astype(bf16), ds.astype(bf16)
 
     refs = ((even_ref, 0), (odd_ref, 0), (even_ref, 1), (odd_ref, 1))
-    dqs = [jnp.zeros((width, lanes), f32) for _ in range(2)]
     pieces = [(0, HALF, (0,))]
     pieces += [(first, HALF, (0, 1)) for first in range(HALF, span, HALF)]
     pieces += [(span, HALF, (1,))]
@@ -211,7 +227,7 @@
         dk = dot(ds, q[used])
         dv = dot(w, g[used])
         for h, x in zip(halves, found):
-            dqs[h] = dqs[h] + dot(kt_scr[:, first : first + rows], x[1])
+            ds_scr[h, first - h * HALF : first - h * HALF + rows, :] = x[1]
         at = slice(first, first + rows)
         k = k_scr[at, :].astype(f32)
         ks_scr[at, :] += dk * k
@@ -227,7 +243,8 @@
             own_ref[0, 0, inner, :] = dk
             own_ref[1, 0, inner, :] = dv
     for h in range(2):
-        dq = (dqs[h] * attn_scale).T
+        dq = dot(kt_scr[:, h * HALF : h * HALF + span], ds_scr[h])
+        dq = (dq * attn_scale).T
         dq_ref[0, h] = dq.reshape(2, HALF, width)
         x = q[h * lanes : (h + 1) * lanes].astype(f32)
         at = slice(h * lanes, (h + 1) * lanes)
@@ -255,46 +272,43 @@
         gain_ref[1:2, :] = key * math.log(2.0)
 
 
-def norm_back(dn, x, gain):
-    inv = lax.rsqrt(jnp.mean(x * x, axis=-1, keepdims=True) + norm_eps)
+def norm_back(x, scaled):
+    inv = inverse(x)
     unit = x * inv
-    gu = dn * gain
-    return inv * (gu - unit * jnp.mean(gu * unit, axis=-1, keepdims=True))
+    return inv * (scaled - unit * row_mean(scaled * unit))
 
 
 def query_end_kernel(q_ref, gain_ref, cos_ref, sin_ref, *rest):
-    dq_refs, out_ref, scr, res = rest[:-3], rest[-3], rest[-2], rest[-1]
+    dq_refs, out_ref, scr = rest[:-2], rest[-2], rest[-1]
     tokens, heads, width = q_ref.shape
-    scr[...] = q_ref[...].astype(f32).reshape(tokens * heads, width)
+    cos, sin, gain = cos_ref[...], sin_ref[...], gain_ref[...]
     head = 0
     for dq_ref in dq_refs:
         for i in range(dq_ref.shape[0]):
             for r in range(2):
                 rows = pl.ds(head, tokens, stride=heads)
-                dn = unturn(dq_ref[i, 0, r], cos_ref[...], sin_ref[...])
-                res[rows, :] = norm_back(dn, scr[rows, :], gain_ref[...])
+                scr[rows, :] = unturn(dq_ref[i, 0, r], cos, sin) * gain
                 head += 1
-    out_ref[...] = res[...].reshape(tokens, heads, width).astype(bf16)
+    out_ref[...] = norm_back(flat(q_ref), scr[...]).reshape(tokens, heads, width).astype(bf16)
 
 
 def key_end_kernel(low_ref, k_ref, gain_ref, cos_ref, sin_ref, *rest):
-    kg_ref, vg_ref, scr, res = rest[-4:]
-    parts = rest[:-4]
+    kg_ref, vg_ref, scr = rest[-3:]
+    parts = rest[:-3]
     tokens, heads, width = k_ref.shape
-    scr[...] = k_ref[...].astype(f32).reshape(tokens * heads, width)
     low = low_ref[0].astype(f32)
+    cos, sin, gain = cos_ref[...], sin_ref[...], gain_ref[...]
     head = 0
     for c in range(len(parts) // 3):
         own, other, came = parts[3 * c : 3 * c + 3]
         for i in range(own.shape[1]):
             rows = pl.ds(head, tokens, stride=heads)
             dk = own[0, i] + other[0, 0, i].astype(f32) * low + came[0, i].astype(f32)
-            dn = unturn(dk, cos_ref[...], sin_ref[...])
-            res[0, rows, :] = norm_back(dn, scr[rows, :], gain_ref[...])
-            res[1, rows, :] = own[1, i] + other[0, 1, i].astype(f32) * low + came[1, i].astype(f32)
+            scr[0, rows, :] = unturn(dk, cos, sin) * gain
+            scr[1, rows, :] = own[1, i] + other[0, 1, i].astype(f32) * low + came[1, i].astype(f32)
             head += 1
-    kg_ref[...] = res[0].reshape(tokens, heads, width).astype(bf16)
-    vg_ref[...] = res[1].reshape(tokens, heads, width).astype(bf16)
+    kg_ref[...] = norm_back(flat(k_ref), scr[0]).reshape(tokens, heads, width).astype(bf16)
+    vg_ref[...] = scr[1].reshape(tokens, heads, width).astype(bf16)
 
 
 def call(kernel, grid, in_specs, out_specs, outs, scratch, cost):
@@ -356,15 +370,16 @@
     for c in range(len(SPLIT)):
         near.append(hop(own[c], 2))
         far.append(hop(near[c], 2))
-        side_own.append(swap(own[c], (0,)))
+        side_own.append(swap(own[c]))
         side_near.append(swap(near[c]))
-        side_far.append(swap(far[c], (1,)))
-
-    starts = (window_start - first + WINDOW_LENGTH).reshape(halves, 1, HALF)
+        side_far.append(swap(far[c]))
+
+    starts = window_start.reshape(halves, 1, HALF)
     qs, go, bias = call(
         query_prep_kernel,
         tokens // TILE,
         [
+            smem,
             q_tile,
             q_tile,
             pl.BlockSpec((1, 1, HALF), lambda i: (i // per_half, 0, 0)),
@@ -380,7 +395,7 @@
         [sds((groups, halves, 2, HALF, width), bf16)] * 2 + [sds((halves, span, HALF), f32)],
         [pltpu.VMEM((2, TILE * heads, width), f32)],
         (16 * mib, 5 * mib),
-    )(queries, output_gradient, starts, query_gain[None, :], cos, sin)
+    )(first.astype(jnp.int32)[None], queries, output_gradient, starts, query_gain[None, :], cos, sin)
 
     kv_spec = pl.BlockSpec((2, 1, tokens, width), lambda i: (0, i, 0, 0))
     term_spec = pl.BlockSpec((2, 2, 1, tokens, width), lambda i: (0, 0, i, 0, 0))
@@ -420,6 +435,7 @@
                 pltpu.VMEM((width, full), bf16),
                 pltpu.VMEM((halves, span, 2 * HALF), f32),
                 pltpu.VMEM((halves, span, 2 * HALF), f32),
+                pltpu.VMEM((halves, span, 2 * HALF), bf16),
                 pltpu.VMEM((full, width), f32),
                 pltpu.VMEM((full, width), f32),
                 pltpu.VMEM((2 * tokens, width), f32),
@@ -448,7 +464,7 @@
         [q_tile, at_rest(1, width), row_spec, row_spec] + [half_spec(n) for n in SPLIT],
         q_tile,
         sds((tokens, heads, width), bf16),
-        [pltpu.VMEM((TILE * heads, width), f32)] * 2,
+        [pltpu.VMEM((TILE * heads, width), f32)],
         (16 * mib, 4 * mib),
     )(queries, query_gain[None, :], cos, sin, *dqs)
     specs = []
@@ -461,10 +477,7 @@
         [smem, kv_tile, at_rest(1, width), row_spec, row_spec] + specs,
         [kv_tile] * 2,
         [sds((tokens, groups, width), bf16)] * 2,
-        [
-            pltpu.VMEM((TILE * groups, width), f32),
-            pltpu.VMEM((2, TILE * groups, width), f32),
-        ],
+        [pltpu.VMEM((2, TILE * groups, width), f32)],
         (8 * mib, 4 * mib),
     )(flag, keys, key_gain[None, :], cos, sin, *ends)
     return query_grad, key_grad, value_grad, gains[0], gains[1]

time: 165 us -> 152 us (0.921)
  starting transfers between devices: 62.2 us -> 52.5 us
  Pallas kernels: 55.7 us -> 46.1 us
  waiting for transfers between devices: 39.5 us -> 45.7 us
    ppermute x8, starting transfers between devices: 10.8 us -> 1.65 us  [swap(): lax.ppermute(value, 'seq', [(s, s ^ 1) for s in range(lax.axis_size('seq'...]
    ppermute x8, waiting for transfers between devices: 34.8 us -> 41 us  [hop(): lax.ppermute(value, 'seq', [(s, s + steps) for s in range(first, last)])]
    pallas_call x1, Pallas kernels: 9.43 us -> 5.4 us  [body(): call(query_end_kernel, tokens // TILE, [q_tile, at_rest(1, width), row_sp...]
    pallas_call x1, Pallas kernels: 9.31 us -> 5.8 us  [body(): call(query_prep_kernel, tokens // TILE, [smem, q_tile, q_tile, pl.BlockSp...]
  transfers between devices with their start and end apart: 28 -> 28, of which waited for: 7 -> 8; matrix products, arithmetic and copies ran while one was open for 1% -> 1% of each run, Pallas kernels for 27% -> 25%
where the time goes in v2:
time: 152 us; the launch traced here: 150 us
  starting transfers between devices  52.5 us (35%)
  Pallas kernels  46.1 us (30%)
  waiting for transfers between devices  45.7 us (30%)
  local copies, waits for them, and re-layouts  2.3 us (2%)
  other arithmetic  2.29 us (2%)
    ppermute x8, waiting for transfers between devices, hop(): lax.ppermute(value, 'seq', [(s, s + steps) for s in range(first, last)])  41 us
    ppermute x8, starting transfers between devices, hop(): lax.ppermute(value, 'seq', [(s, s + steps) for s in range(first, last)])  32 us
    pallas_call x2, Pallas kernels, body(): attend(flag, far[c], near[c], own[c], side_own[c], side_near[c], side_far...  25.7 us
    ppermute x12, starting transfers between devices, all_sum(): lax.ppermute(value, ('seq', 'kv'), list(enumerate(target)))  18.8 us
    pallas_call x1, Pallas kernels, body(): call(query_prep_kernel, tokens // TILE, [smem, q_tile, q_tile, pl.BlockSp...  5.8 us
    pallas_call x1, Pallas kernels, body(): call(query_end_kernel, tokens // TILE, [q_tile, at_rest(1, width), row_sp...  5.4 us
    pallas_call x1, Pallas kernels, body(): call(key_end_kernel, tokens // TILE, [smem, kv_tile, at_rest(1, width), r...  5.09 us
    ppermute x12, waiting for transfers between devices, all_sum(): lax.ppermute(value, ('seq', 'kv'), list(enumerate(target)))  4.67 us
  transfers between devices with their start and end apart: 28, of which 8 were waited for; matrix products, arithmetic and copies ran while one was open for 1% of the time, Pallas kernels for 25%

profile of v2, /device:TPU:24, one launch (start us, length us, event | category | flops | bytes accessed | tf_op | source)
XLA Modules:
  0.0 150.0 jit_solution(8750746066059002720)
XLA Ops:
  0.7 1.2 fusion.6
  1.9 4.1 %shard_map.119 = (bf16[2,4,256,128]{3,2,1,0:T(8,128)(2,1)}, bf16[2,4,256,128]{3,2,1,0:T(8,128)(2,1)}) custom-call(bf16[256,8,128]{2,1,0:T(8,128)(2,1)} %k_ref.3, bf16[256,8,128]{2,1,0:T(8,128)(2,1)} %v_ref.1, f32[1,128]{1,0:T(1,128)} %bitcast.25, f32[256,128]{1,0:T(8,128)} %get-tuple-element.40.cos_ref, f32[256,128]{1,0:T(8,128)} %get-tuple-element.39.sin_ref), custom_call_target="tpu_custom_call" | custom-call | flops 8388608 | bytes 2097152 | tf_op jit(solution)/shard_map/pallas_call | solution.py:360
  6.0 3.8 %collective-permute-start.5 = (bf16[2,4,256,128]{3,2,1,0:T(8,128)(2,1)}, bf16[2,4,256,128]{3,2,1,0:T(8,128)(2,1)S(1)}, u32[]{:S(2)}, u32[]{:S(2)}) collective-permute-start(bf16[2,4,256,128]{3,2,1,0:T(8,128)(2,1)} %get-tuple-element.27.own), channel_id=1, source_target_pairs={{0,4},{2,6},{4,8},{6,10},{8,12},{10,14},{12,16},{14,18},{16,20},{1... | collective-permute-start | bytes 1572872 | tf_op jit(solution)/shard_map/ppermute | solution.py:29
  9.8 3.8 %collective-permute-start = (bf16[2,4,256,128]{3,2,1,0:T(8,128)(2,1)}, bf16[2,4,256,128]{3,2,1,0:T(8,128)(2,1)S(1)}, u32[]{:S(2)}, u32[]{:S(2)}) collective-permute-start(bf16[2,4,256,128]{3,2,1,0:T(8,128)(2,1)} %get-tuple-element.22.own), channel_id=1, source_target_pairs={{0,4},{2,6},{4,8},{6,10},{8,12},{10,14},{12,16},{14,18},{16,20},{1... | collective-permute-start | bytes 1572872 | tf_op jit(solution)/shard_map/ppermute | solution.py:29
  13.6 15.7 %collective-permute-done.5.near = bf16[2,4,256,128]{3,2,1,0:T(8,128)(2,1)S(1)} collective-permute-done((bf16[2,4,256,128]{3,2,1,0:T(8,128)(2,1)}, bf16[2,4,256,128]{3,2,1,0:T(8,128)(2,1)S(1)}, u32[]{:S(2)}, u32[]{:S(2)}) %collective-permute-start.5) | collective-permute-done | bytes 524320 | tf_op jit(solution)/shard_map/ppermute | solution.py:29
  29.4 1.9 %collective-permute-start.6 = (bf16[2,4,256,128]{3,2,1,0:T(8,128)(2,1)S(1)}, bf16[2,4,256,128]{3,2,1,0:T(8,128)(2,1)S(1)}, u32[]{:S(2)}, u32[]{:S(2)}) collective-permute-start(bf16[2,4,256,128]{3,2,1,0:T(8,128)(2,1)S(1)} %collective-permute-done.5.near), channel_id=1, source_target_pairs={{0,4},{2,6},{4,8},{6,10},{8,12},{10,14},{12,16},{14,18},{16,20},{1... | collective-permute-start | bytes 1572872 | tf_op jit(solution)/shard_map/ppermute | solution.py:29
  31.3 0.1 collective-permute-start.7
  31.4 9.2 %collective-permute-done.near = bf16[2,4,256,128]{3,2,1,0:T(8,128)(2,1)S(1)} collective-permute-done((bf16[2,4,256,128]{3,2,1,0:T(8,128)(2,1)}, bf16[2,4,256,128]{3,2,1,0:T(8,128)(2,1)S(1)}, u32[]{:S(2)}, u32[]{:S(2)}) %collective-permute-start) | collective-permute-done | bytes 524320 | tf_op jit(solution)/shard_map/ppermute | solution.py:29
  40.6 1.9 %collective-permute-start.1 = (bf16[2,4,256,128]{3,2,1,0:T(8,128)(2,1)S(1)}, bf16[2,4,256,128]{3,2,1,0:T(8,128)(2,1)S(1)}, u32[]{:S(2)}, u32[]{:S(2)}) collective-permute-start(bf16[2,4,256,128]{3,2,1,0:T(8,128)(2,1)S(1)} %collective-permute-done.near), channel_id=1, source_target_pairs={{0,4},{2,6},{4,8},{6,10},{8,12},{10,14},{12,16},{14,18},{16,20},{1... | collective-permute-start | bytes 1572872 | tf_op jit(solution)/shard_map/ppermute | solution.py:29
  42.5 0.1 collective-permute-start.8
  42.6 9.2 %collective-permute-done.6.far = bf16[2,4,256,128]{3,2,1,0:T(8,128)(2,1)S(1)} collective-permute-done((bf16[2,4,256,128]{3,2,1,0:T(8,128)(2,1)S(1)}, bf16[2,4,256,128]{3,2,1,0:T(8,128)(2,1)S(1)}, u32[]{:S(2)}, u32[]{:S(2)}) %collective-permute-start.6) | collective-permute-done | bytes 524320 | tf_op jit(solution)/shard_map/ppermute | solution.py:29
  51.8 0.5 collective-permute-start.2
  52.3 5.8 %shard_map.120 = (bf16[8,2,2,128,128]{4,3,2,1,0:T(8,128)(2,1)}, bf16[8,2,2,128,128]{4,3,2,1,0:T(8,128)(2,1)}, f32[2,1152,128]{2,1,0:T(8,128)}) custom-call(s32[1]{0:T(128)} %bitcast.3.first_ref, bf16[256,16,128]{2,1,0:T(8,128)(2,1)} %q_ref.3, bf16[256,16,128]{2,1,0:T(8,128)(2,1)} %g_ref.1, s32[2,1,128]{2,1,0:T(1,128)} %bitcast.29, f32[1,128]{1,0:T(1,128)} %bitcast.27, ...), custom_call_target="tpu_custom_call" | custom-call | flops 16777216 | bytes 5242880 | tf_op jit(solution)/shard_map/pallas_call | solution.py:378
  58.2 0.1 collective-permute-start.3
  58.3 3.9 %collective-permute-done.1.far = bf16[2,4,256,128]{3,2,1,0:T(8,128)(2,1)S(1)} collective-permute-done((bf16[2,4,256,128]{3,2,1,0:T(8,128)(2,1)S(1)}, bf16[2,4,256,128]{3,2,1,0:T(8,128)(2,1)S(1)}, u32[]{:S(2)}, u32[]{:S(2)}) %collective-permute-start.1) | collective-permute-done | bytes 524320 | tf_op jit(solution)/shard_map/ppermute | solution.py:29
  62.2 12.9 %shard_map.122 = (bf16[2,2,4,256,128]{4,3,2,1,0:T(8,128)(2,1)}, bf16[2,2,4,256,128]{4,3,2,1,0:T(8,128)(2,1)}, f32[2,4,256,128]{3,2,1,0:T(8,128)}, f32[4,2,2,128,128]{4,3,2,1,0:T(8,128)}, f32[2,128]{1,0:T(2,128)}) custom-call(s32[1]{0:T(128)} %bitcast.1.low_ref, bf16[2,4,256,128]{3,2,1,0:T(8,128)(2,1)} %copy-done.13, bf16[2,4,256,128]{3,2,1,0:T(8,128)(2,1)} %copy-done.11, ...), custom_call_target="tpu_custom_call" | custom-call | flops 6039797760 | bytes 8388608 | tf_op jit(solution)/shard_map/pallas_call | solution.py:446
  75.2 0.5 collective-permute-start.13
  75.7 0.8 copy-done.12
  76.5 12.8 %shard_map.121 = (bf16[2,2,4,256,128]{4,3,2,1,0:T(8,128)(2,1)}, bf16[2,2,4,256,128]{4,3,2,1,0:T(8,128)(2,1)}, f32[2,4,256,128]{3,2,1,0:T(8,128)}, f32[4,2,2,128,128]{4,3,2,1,0:T(8,128)}, f32[2,128]{1,0:T(2,128)}) custom-call(s32[1]{0:T(128)} %bitcast.1.low_ref, bf16[2,4,256,128]{3,2,1,0:T(8,128)(2,1)} %copy-done.10, bf16[2,4,256,128]{3,2,1,0:T(8,128)(2,1)} %copy-done.9, ...), custom_call_target="tpu_custom_call" | custom-call | flops 6039797760 | bytes 8388608 | tf_op jit(solution)/shard_map/pallas_call | solution.py:446
  89.3 0.4 collective-permute-start.10
  89.7 0.7 maximum_multiply_fusion
  90.4 0.6 collective-permute-start.16
  91.0 0.1 collective-permute-start.17
  91.1 1.4 collective-permute-start.18
  92.6 3.6 %collective-permute-start.14 = (bf16[2,4,256,128]{3,2,1,0:T(8,128)(2,1)S(1)}, bf16[2,4,256,128]{3,2,1,0:T(8,128)(2,1)S(1)}, u32[]{:S(2)}, u32[]{:S(2)}) collective-permute-start(bf16[2,4,256,128]{3,2,1,0:T(8,128)(2,1)S(1)} %add_bitcast_fusion), channel_id=1, source_target_pairs={{4,0},{6,2},{8,4},{10,6},{12,8},{14,10},{16,12},{18,14},{20,16},{2... | collective-permute-start | bytes 1572872 | tf_op jit(solution)/shard_map/ppermute | solution.py:29
  96.3 0.1 add_bitcast_fusion.1
  96.4 2.9 %collective-permute-start.11 = (bf16[2,4,256,128]{3,2,1,0:T(8,128)(2,1)S(1)}, bf16[2,4,256,128]{3,2,1,0:T(8,128)(2,1)S(1)}, u32[]{:S(2)}, u32[]{:S(2)}) collective-permute-start(bf16[2,4,256,128]{3,2,1,0:T(8,128)(2,1)S(1)} %add_bitcast_fusion.1), channel_id=1, source_target_pairs={{4,0},{6,2},{8,4},{10,6},{12,8},{14,10},{16,12},{18,14},{20,16},{2... | collective-permute-start | bytes 1572872 | tf_op jit(solution)/shard_map/ppermute | solution.py:29
  99.3 1.1 collective-permute-start.19
  100.4 1.9 %collective-permute-start.21 = (f32[2,128]{1,0:T(2,128)S(1)}, f32[2,128]{1,0:T(2,128)S(1)}, u32[]{:S(2)}, u32[]{:S(2)}) collective-permute-start(f32[2,128]{1,0:T(2,128)S(1)} %add_add_fusion.3), channel_id=1, source_target_pairs={{0,12},{1,13},{2,14},{3,15},{4,16},{5,17},{6,18},{7,19},{8,20},{9,... | collective-permute-start | bytes 3080 | tf_op jit(solution)/shard_map/ppermute | solution.py:52
  102.4 1.8 %collective-permute-done.19 = f32[2,128]{1,0:T(2,128)S(1)} collective-permute-done((f32[2,128]{1,0:T(2,128)S(1)}, f32[2,128]{1,0:T(2,128)S(1)}, u32[]{:S(2)}, u32[]{:S(2)}) %collective-permute-start.19) | collective-permute-done | bytes 1056 | tf_op jit(solution)/shard_map/ppermute | solution.py:52
  104.2 1.9 %collective-permute-done.20 = f32[2,128]{1,0:T(2,128)S(1)} collective-permute-done((f32[2,128]{1,0:T(2,128)S(1)}, f32[2,128]{1,0:T(2,128)S(1)}, u32[]{:S(2)}, u32[]{:S(2)}) %collective-permute-start.20) | collective-permute-done | bytes 1056 | tf_op jit(solution)/shard_map/ppermute | solution.py:52
  106.1 0.9 collective-permute-done.21
  107.0 0.4 collective-permute-start.22
  107.5 0.6 collective-permute-start.23
  108.1 3.7 %collective-permute-start.24 = (f32[2,128]{1,0:T(2,128)S(1)}, f32[2,128]{1,0:T(2,128)S(1)}, u32[]{:S(2)}, u32[]{:S(2)}) collective-permute-start(f32[2,128]{1,0:T(2,128)S(1)} %add_add_fusion.2), channel_id=1, source_target_pairs={{0,192},{1,193},{2,194},{3,195},{4,196},{5,197},{6,198},{7,199},{8... | collective-permute-start | bytes 3080 | tf_op jit(solution)/shard_map/ppermute | solution.py:52
  111.7 0.1 fusion.2
  111.8 5.8 %collective-permute-start.15 = (bf16[2,4,256,128]{3,2,1,0:T(8,128)(2,1)S(1)}, bf16[2,4,256,128]{3,2,1,0:T(8,128)(2,1)S(1)}, u32[]{:S(2)}, u32[]{:S(2)}) collective-permute-start(bf16[2,4,256,128]{3,2,1,0:T(8,128)(2,1)S(1)} %fusion.2), channel_id=1, source_target_pairs={{4,0},{6,2},{8,4},{10,6},{12,8},{14,10},{16,12},{18,14},{20,16},{2... | collective-permute-start | bytes 1572872 | tf_op jit(solution)/shard_map/ppermute | solution.py:29
  117.6 2.9 %collective-permute-done.11 = bf16[2,4,256,128]{3,2,1,0:T(8,128)(2,1)S(1)} collective-permute-done((bf16[2,4,256,128]{3,2,1,0:T(8,128)(2,1)S(1)}, bf16[2,4,256,128]{3,2,1,0:T(8,128)(2,1)S(1)}, u32[]{:S(2)}, u32[]{:S(2)}) %collective-permute-start.11) | collective-permute-done | bytes 524320 | tf_op jit(solution)/shard_map/ppermute | solution.py:29
  120.5 0.1 fusion.5
  120.6 8.2 %collective-permute-start.12 = (bf16[2,4,256,128]{3,2,1,0:T(8,128)(2,1)S(1)}, bf16[2,4,256,128]{3,2,1,0:T(8,128)(2,1)S(1)}, u32[]{:S(2)}, u32[]{:S(2)}) collective-permute-start(bf16[2,4,256,128]{3,2,1,0:T(8,128)(2,1)S(1)} %fusion.5), channel_id=1, source_target_pairs={{4,0},{6,2},{8,4},{10,6},{12,8},{14,10},{16,12},{18,14},{20,16},{2... | collective-permute-start | bytes 1572872 | tf_op jit(solution)/shard_map/ppermute | solution.py:29
  128.9 0.1 collective-permute-start.25
  129.0 0.1 collective-permute-start.26
  129.1 8.8 %collective-permute-start.27 = (f32[2,128]{1,0:T(2,128)S(1)}, f32[2,128]{1,0:T(2,128)S(1)}, u32[]{:S(2)}, u32[]{:S(2)}) collective-permute-start(f32[2,128]{1,0:T(2,128)S(1)} %add_add_fusion.1), channel_id=1, source_target_pairs={{0,48},{1,49},{2,50},{3,51},{4,52},{5,53},{6,54},{7,55},{8,56},{9,... | collective-permute-start | bytes 3080 | tf_op jit(solution)/shard_map/ppermute | solution.py:52
  137.9 5.4 %shard_map.123 = bf16[256,16,128]{2,1,0:T(8,128)(2,1)} custom-call(bf16[256,16,128]{2,1,0:T(8,128)(2,1)} %q_ref.3, f32[1,128]{1,0:T(1,128)} %bitcast.28, f32[256,128]{1,0:T(8,128)} %get-tuple-element.40.cos_ref, f32[256,128]{1,0:T(8,128)} %get-tuple-element.39.sin_ref, f32[4,2,2,128,128]{4,3,2,1,0:T(8,128)} %get-tuple-element.26.rest_0_, ...), custom_call_target="tpu_custom_call" | custom-call | flops 16777216 | bytes 4194304 | tf_op jit(solution)/shard_map/pallas_call | solution.py:461
  143.3 0.5 slice_bitcast_fusion
  143.9 0.8 copy-done.4
  144.6 0.2 copy-done.5
  144.8 5.1 %shard_map.124 = (bf16[256,8,128]{2,1,0:T(8,128)(2,1)}, bf16[256,8,128]{2,1,0:T(8,128)(2,1)}) custom-call(s32[1]{0:T(128)} %bitcast.1.low_ref, bf16[256,8,128]{2,1,0:T(8,128)(2,1)} %k_ref.3, f32[1,128]{1,0:T(1,128)} %bitcast.26, f32[256,128]{1,0:T(8,128)} %get-tuple-element.40.cos_ref, f32[256,128]{1,0:T(8,128)} %get-tuple-element.39.sin_ref, ...), custom_call_target="tpu_custom_call" | custom-call | flops 8388608 | bytes 4194304 | tf_op jit(solution)/shard_map/pallas_call | solution.py:474
  (56 shorter events, 0.2 us)
Async XLA Ops:
  6.0 23.4 %collective-permute-start.5 = (bf16[2,4,256,128]{3,2,1,0:T(8,128)(2,1)}, bf16[2,4,256,128]{3,2,1,0:T(8,128)(2,1)S(1)}, u32[]{:S(2)}, u32[]{:S(2)}) collective-permute-start(bf16[2,4,256,128]{3,2,1,0:T(8,128)(2,1)} %get-tuple-element.27.own), channel_id=1, source_target_pairs={{0,4},{2,6},{4,8},{6,10},{8,12},{10,14},{12,16},{14,18},{16,20},{1... | collective-permute-start | bytes 1572872 | tf_op jit(solution)/shard_map/ppermute | solution.py:29
  9.8 30.8 %collective-permute-start = (bf16[2,4,256,128]{3,2,1,0:T(8,128)(2,1)}, bf16[2,4,256,128]{3,2,1,0:T(8,128)(2,1)S(1)}, u32[]{:S(2)}, u32[]{:S(2)}) collective-permute-start(bf16[2,4,256,128]{3,2,1,0:T(8,128)(2,1)} %get-tuple-element.22.own), channel_id=1, source_target_pairs={{0,4},{2,6},{4,8},{6,10},{8,12},{10,14},{12,16},{14,18},{16,20},{1... | collective-permute-start | bytes 1572872 | tf_op jit(solution)/shard_map/ppermute | solution.py:29
  29.4 28.8 %copy-start.11 = (bf16[2,4,256,128]{3,2,1,0:T(8,128)(2,1)}, bf16[2,4,256,128]{3,2,1,0:T(8,128)(2,1)S(1)}, u32[]{:S(2)}) copy-start(bf16[2,4,256,128]{3,2,1,0:T(8,128)(2,1)S(1)} %collective-permute-done.5.near) | copy-start | bytes 1572868
  29.4 22.5 %collective-permute-start.6 = (bf16[2,4,256,128]{3,2,1,0:T(8,128)(2,1)S(1)}, bf16[2,4,256,128]{3,2,1,0:T(8,128)(2,1)S(1)}, u32[]{:S(2)}, u32[]{:S(2)}) collective-permute-start(bf16[2,4,256,128]{3,2,1,0:T(8,128)(2,1)S(1)} %collective-permute-done.5.near), channel_id=1, source_target_pairs={{0,4},{2,6},{4,8},{6,10},{8,12},{10,14},{12,16},{14,18},{16,20},{1... | collective-permute-start | bytes 1572872 | tf_op jit(solution)/shard_map/ppermute | solution.py:29
  31.3 26.9 %collective-permute-start.7 = (bf16[2,4,256,128]{3,2,1,0:T(8,128)(2,1)}, bf16[2,4,256,128]{3,2,1,0:T(8,128)(2,1)}, u32[]{:S(2)}, u32[]{:S(2)}) collective-permute-start(bf16[2,4,256,128]{3,2,1,0:T(8,128)(2,1)} %get-tuple-element.27.own), channel_id=1, source_target_pairs={{0,2},{2,0},{4,6},{6,4},{8,10},{10,8},{12,14},{14,12},{16,18},{18,... | collective-permute-start | bytes 1572872 | tf_op jit(solution)/shard_map/ppermute | solution.py:33
  40.6 17.6 %copy-start.9 = (bf16[2,4,256,128]{3,2,1,0:T(8,128)(2,1)}, bf16[2,4,256,128]{3,2,1,0:T(8,128)(2,1)S(1)}, u32[]{:S(2)}) copy-start(bf16[2,4,256,128]{3,2,1,0:T(8,128)(2,1)S(1)} %collective-permute-done.near) | copy-start | bytes 1572868
  40.6 21.6 %collective-permute-start.1 = (bf16[2,4,256,128]{3,2,1,0:T(8,128)(2,1)S(1)}, bf16[2,4,256,128]{3,2,1,0:T(8,128)(2,1)S(1)}, u32[]{:S(2)}, u32[]{:S(2)}) collective-permute-start(bf16[2,4,256,128]{3,2,1,0:T(8,128)(2,1)S(1)} %collective-permute-done.near), channel_id=1, source_target_pairs={{0,4},{2,6},{4,8},{6,10},{8,12},{10,14},{12,16},{14,18},{16,20},{1... | collective-permute-start | bytes 1572872 | tf_op jit(solution)/shard_map/ppermute | solution.py:29
  42.5 19.7 %collective-permute-start.8 = (bf16[2,4,256,128]{3,2,1,0:T(8,128)(2,1)S(1)}, bf16[2,4,256,128]{3,2,1,0:T(8,128)(2,1)}, u32[]{:S(2)}, u32[]{:S(2)}) collective-permute-start(bf16[2,4,256,128]{3,2,1,0:T(8,128)(2,1)S(1)} %collective-permute-done.5.near), channel_id=1, source_target_pairs={{0,2},{2,0},{4,6},{6,4},{8,10},{10,8},{12,14},{14,12},{16,18},{18,... | collective-permute-start | bytes 1572872 | tf_op jit(solution)/shard_map/ppermute | solution.py:33
  51.8 6.3 %copy-start.13 = (bf16[2,4,256,128]{3,2,1,0:T(8,128)(2,1)}, bf16[2,4,256,128]{3,2,1,0:T(8,128)(2,1)S(1)}, u32[]{:S(2)}) copy-start(bf16[2,4,256,128]{3,2,1,0:T(8,128)(2,1)S(1)} %collective-permute-done.6.far) | copy-start | bytes 1572868
  51.8 10.4 %collective-permute-start.9 = (bf16[2,4,256,128]{3,2,1,0:T(8,128)(2,1)S(1)}, bf16[2,4,256,128]{3,2,1,0:T(8,128)(2,1)}, u32[]{:S(2)}, u32[]{:S(2)}) collective-permute-start(bf16[2,4,256,128]{3,2,1,0:T(8,128)(2,1)S(1)} %collective-permute-done.6.far), channel_id=1, source_target_pairs={{0,2},{2,0},{4,6},{6,4},{8,10},{10,8},{12,14},{14,12},{16,18},{18,... | collective-permute-start | bytes 1572872 | tf_op jit(solution)/shard_map/ppermute | solution.py:33
  51.8 23.9 %collective-permute-start.2 = (bf16[2,4,256,128]{3,2,1,0:T(8,128)(2,1)}, bf16[2,4,256,128]{3,2,1,0:T(8,128)(2,1)S(1)}, u32[]{:S(2)}, u32[]{:S(2)}) collective-permute-start(bf16[2,4,256,128]{3,2,1,0:T(8,128)(2,1)} %get-tuple-element.22.own), channel_id=1, source_target_pairs={{0,2},{2,0},{4,6},{6,4},{8,10},{10,8},{12,14},{14,12},{16,18},{18,... | collective-permute-start | bytes 1572872 | tf_op jit(solution)/shard_map/ppermute | solution.py:33
  58.2 17.5 %collective-permute-start.3 = (bf16[2,4,256,128]{3,2,1,0:T(8,128)(2,1)S(1)}, bf16[2,4,256,128]{3,2,1,0:T(8,128)(2,1)}, u32[]{:S(2)}, u32[]{:S(2)}) collective-permute-start(bf16[2,4,256,128]{3,2,1,0:T(8,128)(2,1)S(1)} %collective-permute-done.near), channel_id=1, source_target_pairs={{0,2},{2,0},{4,6},{6,4},{8,10},{10,8},{12,14},{14,12},{16,18},{18,... | collective-permute-start | bytes 1572872 | tf_op jit(solution)/shard_map/ppermute | solution.py:33
  62.2 13.0 %copy-start.10 = (bf16[2,4,256,128]{3,2,1,0:T(8,128)(2,1)}, bf16[2,4,256,128]{3,2,1,0:T(8,128)(2,1)S(1)}, u32[]{:S(2)}) copy-start(bf16[2,4,256,128]{3,2,1,0:T(8,128)(2,1)S(1)} %collective-permute-done.1.far) | copy-start | bytes 1572868
  62.2 13.5 %collective-permute-start.4 = (bf16[2,4,256,128]{3,2,1,0:T(8,128)(2,1)S(1)}, bf16[2,4,256,128]{3,2,1,0:T(8,128)(2,1)}, u32[]{:S(2)}, u32[]{:S(2)}) collective-permute-start(bf16[2,4,256,128]{3,2,1,0:T(8,128)(2,1)S(1)} %collective-permute-done.1.far), channel_id=1, source_target_pairs={{0,2},{2,0},{4,6},{6,4},{8,10},{10,8},{12,14},{14,12},{16,18},{18,... | collective-permute-start | bytes 1572872 | tf_op jit(solution)/shard_map/ppermute | solution.py:33
  75.2 14.5 %copy-start.6 = (f32[128]{0:T(128)S(1)}, f32[128]{0:T(128)}, u32[]{:S(2)}) copy-start(f32[128]{0:T(128)} %param.14) | copy-start | bytes 1540
  75.2 14.5 %copy-start.7 = (f32[128]{0:T(128)S(1)}, f32[128]{0:T(128)}, u32[]{:S(2)}) copy-start(f32[128]{0:T(128)} %param.13) | copy-start | bytes 1540
  75.2 14.5 %copy-start.8 = (f32[2,128]{1,0:T(2,128)S(1)}, f32[2,128]{1,0:T(2,128)}, u32[]{:S(2)}) copy-start(f32[2,128]{1,0:T(2,128)} %get-tuple-element.38) | copy-start | bytes 3076
  75.2 17.3 %copy-start.2 = (bf16[2,2,4,256,128]{4,3,2,1,0:T(8,128)(2,1)S(1)}, bf16[2,2,4,256,128]{4,3,2,1,0:T(8,128)(2,1)}, u32[]{:S(2)}) copy-start(bf16[2,2,4,256,128]{4,3,2,1,0:T(8,128)(2,1)} %get-tuple-element.34) | copy-start | bytes 3145732
  75.2 17.3 %collective-permute-start.13 = (bf16[2,2,4,256,128]{4,3,2,1,0:T(8,128)(2,1)}, bf16[2,2,4,256,128]{4,3,2,1,0:T(8,128)(2,1)S(1)}, u32[]{:S(2)}, u32[]{:S(2)}) collective-permute-start(bf16[2,2,4,256,128]{4,3,2,1,0:T(8,128)(2,1)} %get-tuple-element.33), channel_id=1, source_target_pairs={{0,2},{2,0},{4,6},{6,4},{8,10},{10,8},{12,14},{14,12},{16,18},{18,... | collective-permute-start | bytes 3145736 | tf_op jit(solution)/shard_map/ppermute | solution.py:33
  75.7 0.8 copy-start.12
  89.3 7.0 %copy-start.3 = (bf16[2,2,4,256,128]{4,3,2,1,0:T(8,128)(2,1)S(1)}, bf16[2,2,4,256,128]{4,3,2,1,0:T(8,128)(2,1)}, u32[]{:S(2)}) copy-start(bf16[2,2,4,256,128]{4,3,2,1,0:T(8,128)(2,1)} %get-tuple-element.31) | copy-start | bytes 3145732
  89.3 7.0 %collective-permute-start.10 = (bf16[2,2,4,256,128]{4,3,2,1,0:T(8,128)(2,1)}, bf16[2,2,4,256,128]{4,3,2,1,0:T(8,128)(2,1)S(1)}, u32[]{:S(2)}, u32[]{:S(2)}) collective-permute-start(bf16[2,2,4,256,128]{4,3,2,1,0:T(8,128)(2,1)} %get-tuple-element.30), channel_id=1, source_target_pairs={{0,2},{2,0},{4,6},{6,4},{8,10},{10,8},{12,14},{14,12},{16,18},{18,... | collective-permute-start | bytes 3145736 | tf_op jit(solution)/shard_map/ppermute | solution.py:33
  90.4 8.9 %collective-permute-start.16 = (f32[2,128]{1,0:T(2,128)S(1)}, f32[2,128]{1,0:T(2,128)S(1)}, u32[]{:S(2)}, u32[]{:S(2)}) collective-permute-start(f32[2,128]{1,0:T(2,128)S(1)} %maximum_multiply_fusion), channel_id=1, source_target_pairs={{0,1},{1,0},{2,3},{3,2},{4,5},{5,4},{6,7},{7,6},{8,9},{9,8},{10,11... | collective-permute-start | bytes 3080 | tf_op jit(solution)/shard_map/ppermute | solution.py:52
  91.0 8.3 %collective-permute-start.17 = (f32[2,128]{1,0:T(2,128)S(1)}, f32[2,128]{1,0:T(2,128)S(1)}, u32[]{:S(2)}, u32[]{:S(2)}) collective-permute-start(f32[2,128]{1,0:T(2,128)S(1)} %maximum_multiply_fusion), channel_id=1, source_target_pairs={{0,2},{1,3},{2,0},{3,1},{4,6},{5,7},{6,4},{7,5},{8,10},{9,11},{10,... | collective-permute-start | bytes 3080 | tf_op jit(solution)/shard_map/ppermute | solution.py:52
  91.1 8.2 %collective-permute-start.18 = (f32[2,128]{1,0:T(2,128)S(1)}, f32[2,128]{1,0:T(2,128)S(1)}, u32[]{:S(2)}, u32[]{:S(2)}) collective-permute-start(f32[2,128]{1,0:T(2,128)S(1)} %maximum_multiply_fusion), channel_id=1, source_target_pairs={{0,3},{1,2},{2,1},{3,0},{4,7},{5,6},{6,5},{7,4},{8,11},{9,10},{10,... | collective-permute-start | bytes 3080 | tf_op jit(solution)/shard_map/ppermute | solution.py:52
  92.5 19.2 %copy-start = (bf16[2,2,4,256,128]{4,3,2,1,0:T(8,128)(2,1)}, bf16[2,2,4,256,128]{4,3,2,1,0:T(8,128)(2,1)S(1)}, u32[]{:S(2)}) copy-start(bf16[2,2,4,256,128]{4,3,2,1,0:T(8,128)(2,1)S(1)} %collective-permute-done.13.rest_4_) | copy-start | bytes 3145732
  92.6 19.1 %collective-permute-start.14 = (bf16[2,4,256,128]{3,2,1,0:T(8,128)(2,1)S(1)}, bf16[2,4,256,128]{3,2,1,0:T(8,128)(2,1)S(1)}, u32[]{:S(2)}, u32[]{:S(2)}) collective-permute-start(bf16[2,4,256,128]{3,2,1,0:T(8,128)(2,1)S(1)} %add_bitcast_fusion), channel_id=1, source_target_pairs={{4,0},{6,2},{8,4},{10,6},{12,8},{14,10},{16,12},{18,14},{20,16},{2... | collective-permute-start | bytes 1572872 | tf_op jit(solution)/shard_map/ppermute | solution.py:29
  96.3 24.3 %copy-start.1 = (bf16[2,2,4,256,128]{4,3,2,1,0:T(8,128)(2,1)}, bf16[2,2,4,256,128]{4,3,2,1,0:T(8,128)(2,1)S(1)}, u32[]{:S(2)}) copy-start(bf16[2,2,4,256,128]{4,3,2,1,0:T(8,128)(2,1)S(1)} %collective-permute-done.10.rest_1_) | copy-start | bytes 3145732
  96.4 24.2 %collective-permute-start.11 = (bf16[2,4,256,128]{3,2,1,0:T(8,128)(2,1)S(1)}, bf16[2,4,256,128]{3,2,1,0:T(8,128)(2,1)S(1)}, u32[]{:S(2)}, u32[]{:S(2)}) collective-permute-start(bf16[2,4,256,128]{3,2,1,0:T(8,128)(2,1)S(1)} %add_bitcast_fusion.1), channel_id=1, source_target_pairs={{4,0},{6,2},{8,4},{10,6},{12,8},{14,10},{16,12},{18,14},{20,16},{2... | collective-permute-start | bytes 1572872 | tf_op jit(solution)/shard_map/ppermute | solution.py:29
  99.3 4.9 %collective-permute-start.19 = (f32[2,128]{1,0:T(2,128)S(1)}, f32[2,128]{1,0:T(2,128)S(1)}, u32[]{:S(2)}, u32[]{:S(2)}) collective-permute-start(f32[2,128]{1,0:T(2,128)S(1)} %add_add_fusion.3), channel_id=1, source_target_pairs={{0,4},{1,5},{2,6},{3,7},{4,8},{5,9},{6,10},{7,11},{8,12},{9,13},{1... | collective-permute-start | bytes 3080 | tf_op jit(solution)/shard_map/ppermute | solution.py:52
  100.4 5.7 %collective-permute-start.20 = (f32[2,128]{1,0:T(2,128)S(1)}, f32[2,128]{1,0:T(2,128)S(1)}, u32[]{:S(2)}, u32[]{:S(2)}) collective-permute-start(f32[2,128]{1,0:T(2,128)S(1)} %add_add_fusion.3), channel_id=1, source_target_pairs={{0,8},{1,9},{2,10},{3,11},{4,12},{5,13},{6,14},{7,15},{8,16},{9,17... | collective-permute-start | bytes 3080 | tf_op jit(solution)/shard_map/ppermute | solution.py:52
  100.4 6.6 %collective-permute-start.21 = (f32[2,128]{1,0:T(2,128)S(1)}, f32[2,128]{1,0:T(2,128)S(1)}, u32[]{:S(2)}, u32[]{:S(2)}) collective-permute-start(f32[2,128]{1,0:T(2,128)S(1)} %add_add_fusion.3), channel_id=1, source_target_pairs={{0,12},{1,13},{2,14},{3,15},{4,16},{5,17},{6,18},{7,19},{8,20},{9,... | collective-permute-start | bytes 3080 | tf_op jit(solution)/shard_map/ppermute | solution.py:52
  107.0 21.8 %collective-permute-start.22 = (f32[2,128]{1,0:T(2,128)S(1)}, f32[2,128]{1,0:T(2,128)S(1)}, u32[]{:S(2)}, u32[]{:S(2)}) collective-permute-start(f32[2,128]{1,0:T(2,128)S(1)} %add_add_fusion.2), channel_id=1, source_target_pairs={{0,64},{1,65},{2,66},{3,67},{4,68},{5,69},{6,70},{7,71},{8,72},{9,... | collective-permute-start | bytes 3080 | tf_op jit(solution)/shard_map/ppermute | solution.py:52
  107.5 21.4 %collective-permute-start.23 = (f32[2,128]{1,0:T(2,128)S(1)}, f32[2,128]{1,0:T(2,128)S(1)}, u32[]{:S(2)}, u32[]{:S(2)}) collective-permute-start(f32[2,128]{1,0:T(2,128)S(1)} %add_add_fusion.2), channel_id=1, source_target_pairs={{0,128},{1,129},{2,130},{3,131},{4,132},{5,133},{6,134},{7,135},{8... | collective-permute-start | bytes 3080 | tf_op jit(solution)/shard_map/ppermute | solution.py:52
  108.1 20.8 %collective-permute-start.24 = (f32[2,128]{1,0:T(2,128)S(1)}, f32[2,128]{1,0:T(2,128)S(1)}, u32[]{:S(2)}, u32[]{:S(2)}) collective-permute-start(f32[2,128]{1,0:T(2,128)S(1)} %add_add_fusion.2), channel_id=1, source_target_pairs={{0,192},{1,193},{2,194},{3,195},{4,196},{5,197},{6,198},{7,199},{8... | collective-permute-start | bytes 3080 | tf_op jit(solution)/shard_map/ppermute | solution.py:52
  111.8 32.0 %collective-permute-start.15 = (bf16[2,4,256,128]{3,2,1,0:T(8,128)(2,1)S(1)}, bf16[2,4,256,128]{3,2,1,0:T(8,128)(2,1)S(1)}, u32[]{:S(2)}, u32[]{:S(2)}) collective-permute-start(bf16[2,4,256,128]{3,2,1,0:T(8,128)(2,1)S(1)} %fusion.2), channel_id=1, source_target_pairs={{4,0},{6,2},{8,4},{10,6},{12,8},{14,10},{16,12},{18,14},{20,16},{2... | collective-permute-start | bytes 1572872 | tf_op jit(solution)/shard_map/ppermute | solution.py:29
  120.6 23.2 %collective-permute-start.12 = (bf16[2,4,256,128]{3,2,1,0:T(8,128)(2,1)S(1)}, bf16[2,4,256,128]{3,2,1,0:T(8,128)(2,1)S(1)}, u32[]{:S(2)}, u32[]{:S(2)}) collective-permute-start(bf16[2,4,256,128]{3,2,1,0:T(8,128)(2,1)S(1)} %fusion.5), channel_id=1, source_target_pairs={{4,0},{6,2},{8,4},{10,6},{12,8},{14,10},{16,12},{18,14},{20,16},{2... | collective-permute-start | bytes 1572872 | tf_op jit(solution)/shard_map/ppermute | solution.py:29
  128.9 14.4 %collective-permute-start.25 = (f32[2,128]{1,0:T(2,128)S(1)}, f32[2,128]{1,0:T(2,128)S(1)}, u32[]{:S(2)}, u32[]{:S(2)}) collective-permute-start(f32[2,128]{1,0:T(2,128)S(1)} %add_add_fusion.1), channel_id=1, source_target_pairs={{0,16},{1,17},{2,18},{3,19},{4,20},{5,21},{6,22},{7,23},{8,24},{9,... | collective-permute-start | bytes 3080 | tf_op jit(solution)/shard_map/ppermute | solution.py:52
  129.0 14.3 %collective-permute-start.26 = (f32[2,128]{1,0:T(2,128)S(1)}, f32[2,128]{1,0:T(2,128)S(1)}, u32[]{:S(2)}, u32[]{:S(2)}) collective-permute-start(f32[2,128]{1,0:T(2,128)S(1)} %add_add_fusion.1), channel_id=1, source_target_pairs={{0,32},{1,33},{2,34},{3,35},{4,36},{5,37},{6,38},{7,39},{8,40},{9,... | collective-permute-start | bytes 3080 | tf_op jit(solution)/shard_map/ppermute | solution.py:52
  129.1 14.2 %collective-permute-start.27 = (f32[2,128]{1,0:T(2,128)S(1)}, f32[2,128]{1,0:T(2,128)S(1)}, u32[]{:S(2)}, u32[]{:S(2)}) collective-permute-start(f32[2,128]{1,0:T(2,128)S(1)} %add_add_fusion.1), channel_id=1, source_target_pairs={{0,48},{1,49},{2,50},{3,51},{4,52},{5,53},{6,54},{7,55},{8,56},{9,... | collective-permute-start | bytes 3080 | tf_op jit(solution)/shard_map/ppermute | solution.py:52
  143.8 0.8 copy-start.4
  143.9 1.0 copy-start.5
